TPU v7x, 128 devices: a whole 4x4x4 slice. The times are simulated.
128 devices in a mesh: gx: 16 (over y, x_hi, core), gy: 8 (over x_lo, z).
Axes of the slice: x: 4 (x_hi: 2, x_lo: 2; x = x_hi * 2 + x_lo), y: 4, z: 4, core: 2. Of those that a mesh axis runs over, the one named last changes fastest.
Arguments:
- ocean_depth: float32 [4096, 4096], P('gx', 'gy'), may hold values from 0.5 to 8
- wet_mask: int32 [4096, 4096], P('gx', 'gy'), may hold values 0 or 1
- manning: float32 [4096, 4096], P('gx', 'gy'), may hold values from 0.5 to 5
- fault_slip: float32 [2048], P(('gx', 'gy')), may hold values from 0.3 to 1.2
- pattern: float32 [32768, 8, 128], P(('gx', 'gy')), may hold values from -1 to 1
- foot_tile: int32 [32768, 1], P(('gx', 'gy')), may hold values from 0 to 127; in each aligned block of 256 rows (0 to 255, 256 to 511, ...) at most 4 rows name the same one
- foot_block: int32 [32768], P(('gx', 'gy')), may hold values from 0 to 127
- gauge_row: int32 [2048], replicated, may hold values from 0 to 4095, as said below
- gauge_col: int32 [2048], replicated, may hold values from 0 to 4095, as said below
- observed: float32 [4, 2048], replicated, may hold values from -6 to 6
Outputs:
- final_eta: float32 [4096, 4096], P('gx', 'gy')
- readings: float32 [4, 2048], replicated
- source_adjoint: float32 [4096, 4096], P('gx', 'gy')
- grad_slip: float32 [2048], P(('gx', 'gy'))
Inputs may be any that keep to these rules, and one draw needn't show every extreme that they name: `foot_tile`: the 256 rows of one device name no tile more than 4 times, a bound that some block reaches. Tile t is the one at tile row t // 8 and tile column t % 8. `gauge_row`: gauges 16 * t to 16 * t + 15 lie in tile t, within three cells of one of its edges. `gauge_col`: see gauge_row.
All inputs are finite; a program needn't handle non-finite values. No bound on the sum of `wet_mask` on one device may be relied on, other than what follows from the above.
Results may differ from a plain program's by a relative error of at most 0.0003.
Values sent between devices are 32-bit elements; how exact they have to be, the bound alone decides.
No kernel may reach another device: no remote copies, remote signals or barrier semaphores. Data moves between devices by JAX's collectives and lax.ppermute only.
A program may use at most 128 MiB of HBM per device.

v0:
```python
import math

import jax
import jax.numpy as jnp
from jax import lax
from jax.experimental import pallas as pl
from jax.experimental.pallas import tpu as pltpu
from jax.sharding import PartitionSpec as P

wave_gain = 0.2
mass_gain = 0.2
min_depth = 0.25
speed_floor = 0.01

HALO = 8
CHUNK = 33
SLOTS = 4
LN2 = math.log(2.0)
PUSH = -0.5 * wave_gain
assert abs(PUSH * PUSH - speed_floor) < 1e-12
ROUGH_SCALE = 0.5 * abs(PUSH) * 2.0 ** (7.0 / 3.0)
F32 = jnp.float32
MIB = 1 << 20
UNROLL = 4
I32 = jnp.int32


def vmem():
    return pl.BlockSpec(memory_space=pltpu.VMEM)


def smem():
    return pl.BlockSpec(memory_space=pltpu.SMEM)


def hbm():
    return pl.BlockSpec(memory_space=pl.ANY)


def shifted(shard, axis, by):
    devices = lax.axis_size(axis)
    pairs = [(i, i + by) for i in range(devices) if 0 <= i + by < devices]
    return lax.ppermute(shard, axis, pairs)


def pack_kernel(
    slip_ref, tile_ref, block_ref, pattern_hbm, out_ref, table_ref, pattern, row_v, row_s, sems
):
    load = pltpu.make_async_copy(pattern_hbm, pattern, sems.at[0])
    load.start()
    rows = out_ref.shape[0]
    tiles = rows // CHUNK
    entries = tile_ref.shape[1]
    faults = slip_ref.shape[0]
    per_fault = entries // faults
    tile_row = tile_ref[...]
    tile_f = tile_row.astype(F32)
    tile_col = jnp.broadcast_to(tile_f, (128, entries)).T
    here = lax.broadcasted_iota(I32, (entries, 128), 0)
    ranks = []
    for q in range(entries // 128):
        there = lax.broadcasted_iota(I32, (entries, 128), 1) + q * 128
        same = (tile_col == tile_f[:, q * 128 : q * 128 + 128]) & (here < there)
        ranks.append(jnp.sum(jnp.where(same, 1.0, 0.0), axis=0, keepdims=True))
    rank = jnp.concatenate(ranks, axis=1).astype(I32)
    row_v[...] = tile_row * CHUNK + rank * 8
    place_rows = pltpu.make_async_copy(row_v, row_s, sems.at[1])
    place_rows.start()
    fault = lax.broadcasted_iota(I32, (1, entries), 1) // per_fault
    slot = lax.broadcasted_iota(I32, (128, entries), 0)
    facts = jnp.where(slot == rank, block_ref[...], 0) + jnp.where(slot == rank + 8, fault + 1, 0)
    hot = jnp.where(lax.broadcasted_iota(I32, (tiles, entries), 0) == tile_row, 1.0, 0.0)
    table_ref[...] = lax.dot_general(
        hot.astype(jnp.bfloat16),
        facts.astype(F32).astype(jnp.bfloat16),
        (((1,), (1,)), ((), ())),
        preferred_element_type=F32,
    )
    zero = jnp.zeros((8, 128), F32)

    def clear(i, c):
        out_ref[pl.ds(pl.multiple_of(i * 8, 8), 8), :] = zero
        return c

    lax.fori_loop(0, rows // 8, clear, 0, unroll=16)
    for t in range(tiles):
        out_ref[t * CHUNK + 32 : t * CHUNK + 33, :] = table_ref[t : t + 1, :]
    place_rows.wait()
    load.wait()

    def place(s, c):
        slip = slip_ref[s]
        for j in range(per_fault):
            i = s * per_fault + j
            out_ref[pl.ds(row_s[0, i], 8), :] = pattern[i] * slip
        return c

    lax.fori_loop(0, faults, place, 0)


def edges_of(first, last):
    lane = lax.broadcasted_iota(I32, first.shape, 1)
    both = jnp.where(lane < 64, first, last).T
    return both[0:8], both[120:128]


def side_block(east, west):
    rows = east.shape[1]
    gap = jnp.zeros((128 - 16, rows), F32)
    return jnp.concatenate([east, gap, west], axis=0).T


def meta_copy(meta_hbm, meta, sem):
    return pltpu.make_async_copy(meta_hbm.at[:, :, pl.ds(8 * SLOTS * 128, 128)], meta, sem)


def scatter_kernel(
    meta_hbm, recv_ref, wet_ref, west_in, east_in, top_in, bottom_in, after,
    eta_ref, west_ref, east_ref, top_ref, bottom_ref, meta, sem, *acc,
):
    del after
    load = meta_copy(meta_hbm, meta, sem)
    load.start()
    tiles = recv_ref.shape[0] // CHUNK
    rows, cols = eta_ref.shape
    across = cols // 128
    zero = jnp.zeros((8, 128), F32)

    def clear(i, c):
        for a in acc:
            a[i] = zero
        return c

    lax.fori_loop(0, acc[0].shape[0], clear, 0, unroll=8)
    for dst, src in (
        (west_ref, west_in), (east_ref, east_in), (top_ref, top_in), (bottom_ref, bottom_in)
    ):
        dst[0:24, :] = src[...]
    load.wait()

    def add(i, c):
        base = pl.multiple_of(i * (8 * CHUNK), 8)
        for u in range(8):
            for j in range(SLOTS):
                b = meta[i * 8 + u, 0, j].astype(I32)
                acc[j][b] = acc[j][b] + recv_ref[pl.ds(base + (u * CHUNK + 8 * j), 8), :]
        return c

    lax.fori_loop(0, tiles // 8, add, 0)

    def merge(i, c):
        r = pl.multiple_of(i * 8, 8)
        for q in range(across):
            b = i * across + q
            total = (acc[0][b] + acc[1][b]) + (acc[2][b] + acc[3][b])
            wet = wet_ref[pl.ds(r, 8), q * 128 : q * 128 + 128].astype(F32)
            eta_ref[pl.ds(r, 8), q * 128 : q * 128 + 128] = total * wet
        return c

    lax.fori_loop(0, rows // 8, merge, 0, unroll=2)
    west, east = edges_of(eta_ref[:, 0:128], eta_ref[:, cols - 128 : cols])
    west_ref[24:32] = west
    east_ref[24:32] = east
    top_ref[24:32] = eta_ref[0:8, :]
    bottom_ref[24:32] = eta_ref[rows - 8 : rows, :]


def static_edge_kernel(
    depth_ref, wet_ref, fric_ref, west_ref, east_ref, top_ref, bottom_ref
):
    rows, cols = depth_ref.shape
    for n, ref in enumerate((depth_ref, wet_ref, fric_ref)):
        at = slice(8 * n, 8 * n + 8)
        west, east = edges_of(ref[:, 0:128].astype(F32), ref[:, cols - 128 : cols].astype(F32))
        west_ref[at] = west
        east_ref[at] = east
        top_ref[at] = ref[0:8, :].astype(F32)
        bottom_ref[at] = ref[rows - 8 : rows, :].astype(F32)


def rim_kernel(east_ref, west_ref, top_in, bottom_in, top_ref, bottom_ref):
    fields = east_ref.shape[0] // 8
    rows = east_ref.shape[1]
    cols = top_in.shape[1]
    lane = lax.broadcasted_iota(I32, (8, 128), 1)
    for src, out, first, keep in (
        (top_in, top_ref, 0, slice(0, 8)),
        (bottom_in, bottom_ref, rows - 128, slice(120, 128)),
    ):
        pieces = []
        for n in range(fields):
            at = slice(8 * n, 8 * n + 8)
            pieces += [west_ref[at, first : first + 128], east_ref[at, first : first + 128]]
        pieces.append(jnp.zeros((128 - 16 * fields, 128), F32))
        corners = jnp.concatenate(pieces, axis=0).T[keep]
        for n in range(fields):
            at = slice(8 * n, 8 * n + 8)
            out[at, 0:cols] = src[at, :]
            out[at, cols:] = jnp.where(
                (lane < 8) | (lane >= 120), pltpu.roll(corners, 128 - 16 * n - 8, 1), 0.0
            )


def assemble(out, n, ref, east_ref, west_ref, north_ref, south_ref):
    rows, cols = ref.shape
    at = slice(8 * n, 8 * n + 8)
    out[0:8, :] = north_ref[at]
    out[8 : 8 + rows, 0:cols] = ref[...].astype(F32)
    out[8 : 8 + rows, cols:] = side_block(east_ref[at], west_ref[at])
    out[8 + rows : 16 + rows, :] = south_ref[at]


def row_iota(shape):
    return lax.broadcasted_iota(I32, shape, 0)


def gauge_kernel(place_ref, row_ref, col_ref, obs_ref, count_out, obs_out):
    steps, rows, cols = obs_out.shape
    own_rows = rows - 2 * HALO
    own_cols = cols - 128
    gx, gy, wx, wy = place_ref[0], place_ref[1], place_ref[2], place_ref[3]
    per = row_ref.shape[0] // (wx * wy)
    zero = jnp.zeros((8, cols), F32)

    def clear(i, c):
        r = pl.multiple_of(i * 8, 8)
        count_out[pl.ds(r, 8), :] = zero
        for k in range(steps):
            obs_out[k, pl.ds(r, 8), :] = zero
        return c

    lax.fori_loop(0, rows // 8, clear, 0)
    sub = row_iota((8, 128))
    lane = lax.broadcasted_iota(I32, (8, 128), 1)

    for dx in (-1, 0, 1):
        for dy in (-1, 0, 1):
            tx = gx + dx
            ty = gy + dy
            inside = (tx >= 0) & (tx < wx) & (ty >= 0) & (ty < wy)
            first = jnp.where(inside, (tx * wy + ty) * per, 0)

            def one(g, c, first=first, inside=inside):
                r = row_ref[first + g] - gx * own_rows + HALO
                q = col_ref[first + g] - gy * own_cols
                ok = inside & (r >= 0) & (r < rows) & (q >= -HALO) & (q < own_cols + HALO)
                q = jnp.where(q < 0, q + cols, q)

                @pl.when(ok)
                def _():
                    rb = pl.multiple_of(r // 8 * 8, 8)
                    cb = pl.multiple_of(q // 128 * 128, 128)
                    hit = (sub == r % 8) & (lane == q % 128)
                    at = (pl.ds(rb, 8), pl.ds(cb, 128))
                    count_out[at] = count_out[at] + jnp.where(hit, 1.0, 0.0)
                    for k in range(steps):
                        at_k = (k,) + at
                        obs_out[at_k] = obs_out[at_k] + jnp.where(hit, obs_ref[k, first + g], 0.0)

                return c

            lax.fori_loop(0, per, one, 0)


def face(f, s, sn, dd, rr, ww):
    x = dd + (s + sn)
    total = jnp.maximum(x, 2.0 * min_depth)
    diff = sn - s
    push = total * diff
    if f is not None:
        push = push + f
    t = push * push + 1.0
    y = (rr * jnp.exp2(jnp.log(total) * (-7.0 / 3.0 / LN2))) * lax.rsqrt(t)
    inv = 1.0 / (t * y + 1.0)
    wi = ww * inv
    flux = wi * push
    a = (wi * inv) * (y + 1.0)
    depth_part = (flux - flux * inv) * ((7.0 / 3.0) / total)
    share = jnp.where(
        x > 2.0 * min_depth, 1.0, jnp.where(x == 2.0 * min_depth, 0.5, 0.0)
    )
    u = share * (depth_part + a * diff)
    v = a * total
    return flux, a, u + v, u - v


def merge_rows(tiles):
    sub = row_iota((8, 128))
    for width in (1, 2, 4):
        low = (sub & width) == 0
        tiles = [
            jnp.where(low, p, q) + pltpu.roll(jnp.where(low, q, p), width, 0)
            for p, q in zip(tiles[0::2], tiles[1::2])
        ]
    return tiles[0]


def solve_kernel(
    place_ref, grow_ref, gcol_ref,
    eta_ref, depth_ref, wet_ref, fric_ref, east_ref, west_ref, north_ref, south_ref,
    count, obs, recv, meta_hbm,
    final_ref, adj_ref, back_ref,
    depth_x, wet, fric_x, dde, dds, rre, rrs, wwe, wws,
    surf, fe, fs, ae, pe, qe, as_, ps, qs, adj, ce, cs, grads,
    parts, reads, meta, sem,
):
    steps, rows, cols = obs.shape
    own_rows, own_cols = eta_ref.shape
    load = meta_copy(meta_hbm, meta, sem)
    load.start()
    halos = (east_ref, west_ref, north_ref, south_ref)
    assemble(depth_x, 0, depth_ref, *halos)
    assemble(wet, 1, wet_ref, *halos)
    assemble(fric_x, 2, fric_ref, *halos)
    assemble(surf.at[0], 3, eta_ref, *halos)
    sub = row_iota((8, cols))
    last = sub == 7
    firstrow = sub == 0
    blocks = rows // 8
    across = own_cols // 128

    def nxt(i):
        return pl.multiple_of(jnp.minimum(i * 8 + 8, rows - 8), 8)

    for k in range(steps):

        def eastward(i, c, k=k):
            here = pl.ds(pl.multiple_of(i * 8, 8), 8)
            if k == 0:
                d, w, m = depth_x[here, :], wet[here, :], fric_x[here, :]
                dde[here, :] = d + pltpu.roll(d, cols - 1, 1)
                wwe[here, :] = w * pltpu.roll(w, cols - 1, 1)
                rre[here, :] = ROUGH_SCALE * (m + pltpu.roll(m, cols - 1, 1))
            s = surf[k, here, :]
            old = None if k == 0 else fe[here, :]
            flux, a, p, q = face(
                old, s, pltpu.roll(s, cols - 1, 1), dde[here, :], rre[here, :], wwe[here, :]
            )
            fe[here, :] = flux
            if k > 0:
                ae[k - 1, here, :] = a
            pe[k, here, :] = p
            qe[k, here, :] = q
            return c

        def southward(i, carry, k=k):
            s, s_up, f_down = carry
            here = pl.ds(pl.multiple_of(i * 8, 8), 8)
            after = pl.ds(nxt(i), 8)
            if k == 0:

                def south(ref):
                    return jnp.where(last, pltpu.roll(ref[after, :], 7, 0), pltpu.roll(ref[here, :], 7, 0))

                dds[here, :] = depth_x[here, :] + south(depth_x)
                wws[here, :] = wet[here, :] * south(wet)
                rrs[here, :] = ROUGH_SCALE * (fric_x[here, :] + south(fric_x))
            sn = surf[k, after, :]
            sn_up = pltpu.roll(sn, 7, 0)
            old = None if k == 0 else fs[here, :]
            flux, a, p, q = face(
                old, s, jnp.where(last, sn_up, s_up), dds[here, :], rrs[here, :], wws[here, :]
            )
            fs[here, :] = flux
            if k > 0:
                as_[k - 1, here, :] = a
            ps[k, here, :] = p
            qs[k, here, :] = q
            down = pltpu.roll(flux, 1, 0)
            east = fe[here, :]
            div = east - pltpu.roll(east, 1, 1)
            div = div + (flux - jnp.where(firstrow, f_down, down))
            surf[k + 1, here, :] = wet[here, :] * (s - (mass_gain * PUSH) * div)
            return sn, sn_up, down

        s0 = surf[k, 0:8, :]
        lax.fori_loop(0, blocks, eastward, 0, unroll=UNROLL)
        lax.fori_loop(
            0,
            blocks,
            southward,
            (s0, pltpu.roll(s0, 7, 0), jnp.zeros((8, cols), F32)),
            unroll=UNROLL,
        )

    final_ref[...] = surf[steps, HALO : HALO + own_rows, 0:own_cols]

    gx, gy = place_ref[0], place_ref[1]
    lane8 = lax.broadcasted_iota(I32, (8, 128), 1)
    sub8 = row_iota((8, 128))
    per = grow_ref.shape[0] // (place_ref[2] * place_ref[3])
    per_tile = reads.shape[0] // steps
    first = (gx * place_ref[3] + gy) * per
    for g0 in range(0, per_tile, 8):
        spots = []
        for g in range(g0, g0 + 8):
            r = jnp.clip(grow_ref[first + g] - gx * own_rows, 0, own_rows - 1) + HALO
            q = jnp.clip(gcol_ref[first + g] - gy * own_cols, 0, own_cols - 1)
            at = (
                pl.ds(pl.multiple_of(r // 8 * 8, 8), 8),
                pl.ds(pl.multiple_of(q // 128 * 128, 128), 128),
            )
            spots.append((at, (sub8 == r % 8) & (lane8 == q % 128)))
        for k in range(steps):
            picked = [jnp.where(hit, surf[(k + 1,) + at], 0.0) for at, hit in spots]
            reads[k * per_tile + g0 : k * per_tile + g0 + 8, :] = merge_rows(picked)
    values = jnp.sum(reads[...], axis=1, keepdims=True)
    spots = row_iota(reads.shape) + SLOTS == lax.broadcasted_iota(I32, reads.shape, 1)
    reading_row = jnp.sum(jnp.where(spots, values, 0.0), axis=0, keepdims=True)

    load.wait()

    for k in reversed(range(steps)):

        def seeded(value, at, k):
            seed = count[at, :] * surf[k + 1, at, :] - obs[k, at, :]
            return seed if value is None else value + seed

        def b_of(r, k=k):
            at = pl.ds(r, 8)
            a = seeded(None, at, k) if k == steps - 1 else adj[at, :]
            return wet[at, :] * a

        def backward(i, carry, k=k):
            b, b_up, x_down = carry
            r = pl.multiple_of(i * 8, 8)
            here = pl.ds(r, 8)
            bn = b_of(nxt(i))
            bn_up = pltpu.roll(bn, 7, 0)
            b_south = jnp.where(last, bn_up, b_up)
            b_east = pltpu.roll(b, cols - 1, 1)
            ge = (mass_gain * PUSH) * (b_east - b)
            gs = (mass_gain * PUSH) * (b_south - b)
            if k < steps - 1:
                ge = ge + ce[here, :]
                gs = gs + cs[here, :]
            if k > 0:
                ce[here, :] = ge * ae[k - 1, here, :]
                cs[here, :] = gs * as_[k - 1, here, :]
            xe = ge * pe[k, here, :]
            xs = gs * ps[k, here, :]
            down = pltpu.roll(xs, 1, 0)
            out = b + ge * qe[k, here, :] + pltpu.roll(xe, 1, 1)
            out = out + gs * qs[k, here, :] + jnp.where(firstrow, x_down, down)
            if k > 0:
                out = seeded(out, here, k - 1)
            adj[here, :] = out
            if k == 0:
                scaled = out * wet[here, :]
                for q in range(across):
                    grads[i * across + q] = scaled[:, q * 128 : q * 128 + 128]
            return bn, bn_up, down

        b0 = b_of(0)
        lax.fori_loop(
            0,
            blocks,
            backward,
            (b0, pltpu.roll(b0, 7, 0), jnp.zeros((8, cols), F32)),
            unroll=2,
        )

    adj_ref[...] = adj[HALO : HALO + own_rows, 0:own_cols]

    tiles = recv.shape[0] // CHUNK

    def sens(i, c):
        for j in range(SLOTS):
            products = []
            for u in range(8):
                t = i * 8 + u
                b = meta[t, 0, j].astype(I32) + HALO // 8 * across
                products.append(grads[b] * recv[pl.ds(t * CHUNK + 8 * j, 8), :])
            parts[j, pl.ds(pl.multiple_of(i * 8, 8), 8), :] = merge_rows(products)
        return c

    lax.fori_loop(0, tiles // 8, sens, 0)
    lanes = lax.broadcasted_iota(I32, (tiles, 128), 1)
    out = jnp.broadcast_to(reading_row, (tiles, 128))
    for j in range(SLOTS):
        out = jnp.where(lanes == j, jnp.sum(parts[j], axis=1, keepdims=True), out)
    back_ref[...] = out


def body(
    ocean_depth,
    wet_mask,
    manning,
    fault_slip,
    pattern,
    foot_tile,
    foot_block,
    gauge_row,
    gauge_col,
    observed,
):
    rows_here, cols_here = ocean_depth.shape
    steps, gauges = observed.shape
    width_x = lax.axis_size("gx")
    width_y = lax.axis_size("gy")
    devices = width_x * width_y
    entries = pattern.shape[0]
    faults = fault_slip.shape[0]
    per_fault = entries // faults
    per_tile = gauges // devices
    both = ("gx", "gy")
    rows, cols = rows_here + 2 * HALO, cols_here + 128
    f = jax.ShapeDtypeStruct

    packed, table = pl.pallas_call(
        pack_kernel,
        out_shape=[f((devices * CHUNK, 128), F32), f((devices, 128), F32)],
        in_specs=[smem(), vmem(), vmem(), hbm()],
        out_specs=[vmem()] * 2,
        scratch_shapes=[
            pltpu.VMEM(pattern.shape, F32),
            pltpu.VMEM((1, entries), I32),
            pltpu.SMEM((1, entries), I32),
            pltpu.SemaphoreType.DMA((2,)),
        ],
        name="pack",
    )(fault_slip, foot_tile.reshape(1, entries), foot_block.reshape(1, entries), pattern)
    recv_flat = lax.all_to_all(packed.reshape(-1), both, split_axis=0, concat_axis=0, tiled=True)
    recv = recv_flat.reshape(devices * CHUNK, 128)

    edge = [f((24, rows_here), F32)] * 2 + [f((24, cols_here), F32)] * 2
    edges = pl.pallas_call(
        static_edge_kernel,
        out_shape=edge,
        in_specs=[vmem()] * 3,
        out_specs=[vmem()] * 4,
        name="static_edges",
        compiler_params=pltpu.CompilerParams(vmem_limit_bytes=4 * MIB),
    )(ocean_depth, wet_mask, manning)
    grid = f((rows, cols), F32)
    place = jnp.stack(
        [lax.axis_index("gx"), lax.axis_index("gy"), jnp.int32(width_x), jnp.int32(width_y)]
    ).astype(I32)
    count, obs = pl.pallas_call(
        gauge_kernel,
        out_shape=[grid, f((steps, rows, cols), F32)],
        in_specs=[smem()] * 4,
        out_specs=[vmem()] * 2,
        name="gauges",
        compiler_params=pltpu.CompilerParams(vmem_limit_bytes=2 * MIB),
    )(place, gauge_row, gauge_col, observed)

    slots_view = recv_flat.reshape(devices, 1, CHUNK * 128)
    eta, west, east, top, bottom = pl.pallas_call(
        scatter_kernel,
        out_shape=[f((rows_here, cols_here), F32)]
        + [f((32, rows_here), F32)] * 2
        + [f((32, cols_here), F32)] * 2,
        in_specs=[hbm()] + [vmem()] * 6 + [hbm()],
        out_specs=[vmem()] * 5,
        scratch_shapes=[pltpu.SMEM((devices, 1, 128), F32), pltpu.SemaphoreType.DMA]
        + [pltpu.VMEM((rows_here * cols_here // 1024, 8, 128), F32)] * SLOTS,
        name="scatter",
        compiler_params=pltpu.CompilerParams(vmem_limit_bytes=10 * MIB),
    )(slots_view, recv, wet_mask, *edges, count)
    from_east = shifted(west, "gy", -1)
    from_west = shifted(east, "gy", 1)
    top, bottom = pl.pallas_call(
        rim_kernel,
        out_shape=[f((32, cols), F32)] * 2,
        in_specs=[vmem()] * 4,
        out_specs=[vmem()] * 2,
        name="rims",
        compiler_params=pltpu.CompilerParams(vmem_limit_bytes=2 * MIB),
    )(from_east, from_west, top, bottom)
    from_south = shifted(top, "gx", -1)
    from_north = shifted(bottom, "gx", 1)

    tile = f((rows_here, cols_here), F32)
    scratch = pltpu.VMEM((rows, cols), F32)
    final, adjoint, back = pl.pallas_call(
        solve_kernel,
        out_shape=[tile, tile, f((devices, 128), F32)],
        in_specs=[smem()] * 3 + [vmem()] * 11 + [hbm()],
        out_specs=[vmem()] * 3,
        scratch_shapes=[scratch] * 9
        + [
            pltpu.VMEM((steps + 1, rows, cols), F32),
            scratch,
            scratch,
            pltpu.VMEM((steps - 1, rows, cols), F32),
            pltpu.VMEM((steps, rows, cols), F32),
            pltpu.VMEM((steps, rows, cols), F32),
            pltpu.VMEM((steps - 1, rows, cols), F32),
            pltpu.VMEM((steps, rows, cols), F32),
            pltpu.VMEM((steps, rows, cols), F32),
            scratch,
            scratch,
            scratch,
            pltpu.VMEM((rows // 8 * (cols_here // 128), 8, 128), F32),
            pltpu.VMEM((SLOTS, devices, 128), F32),
            pltpu.VMEM((steps * per_tile, 128), F32),
            pltpu.SMEM((devices, 1, 128), F32),
            pltpu.SemaphoreType.DMA,
        ],
        name="solve",
        compiler_params=pltpu.CompilerParams(vmem_limit_bytes=44 * MIB),
    )(
        place, gauge_row, gauge_col,
        eta, ocean_depth, wet_mask, manning, from_east, from_west, from_north, from_south,
        count, obs, recv, slots_view,
    )
    returned = lax.all_to_all(back, both, split_axis=0, concat_axis=0, tiled=True)
    readings = (
        returned[:, SLOTS : SLOTS + steps * per_tile]
        .reshape(devices, steps, per_tile)
        .transpose(1, 0, 2)
        .reshape(steps, gauges)
    )
    fault_of = table[:, 8 : 8 + SLOTS].astype(I32) - 1
    mine = fault_of[:, :, None] == jnp.arange(faults, dtype=I32)[None, None, :]
    grad_slip = (
        jnp.sum(jnp.where(mine, returned[:, :SLOTS, None], 0.0), axis=(0, 1)) / fault_slip
    )
    return (final, readings, adjoint, grad_slip)


def solution(mesh):
    placed = (
        P("gx", "gy"),
        P("gx", "gy"),
        P("gx", "gy"),
        P(("gx", "gy")),
        P(("gx", "gy"), None, None),
        P(("gx", "gy"), None),
        P(("gx", "gy")),
        P(),
        P(),
        P(),
    )
    return jax.shard_map(
        body,
        mesh=mesh,
        in_specs=placed,
        out_specs=(P("gx", "gy"), P(), P("gx", "gy"), P(("gx", "gy"))),
        check_vma=False,
    )
```

profile of v0, /device:TPU:1, one launch (start us, length us, event | category | flops | bytes accessed | tf_op | source)
XLA Modules:
  0.0 121.1 jit_solution(4070292701852948042)
XLA Ops:
  0.6 3.6 %pack.1 = (f32[4224,128]{1,0:T(8,128)}, f32[128,128]{1,0:T(8,128)}) custom-call(f32[16]{0:T(128)} %slip_ref.1, s32[1,256]{1,0:T(1,128)} %bitcast.22, s32[1,256]{1,0:T(1,128)} %bitcast.23, f32[256,8,128]{2,1,0:T(8,128)} %pattern_hbm.1), custom_call_target="tpu_custom_call" | custom-call | tf_op jit(solution)/shard_map/pack/pallas_call | solution.py:510
  4.3 0.0 copy-start
  4.3 0.0 copy-start.3
  4.3 0.0 copy-start.9
  4.3 11.5 %all-to-all-start = ((f32[128,4224,1]{1,2,0:T(1,128)}), f32[128,4224,1]{1,2,0:T(1,128)S(1)}, u32[]{:S(2)}, u32[]{:S(2)}) async-start(f32[128,4224,1]{1,2,0:T(1,128)} %bitcast.18), calls=%async_computation | async-start | bytes 4325376 | tf_op jit(solution)/shard_map/all_to_all | solution.py:523
  15.9 1.0 copy-done.5
  16.9 0.1 static_edges.1
  17.1 0.6 copy-done.10
  17.7 0.1 pad_add_fusion.place_ref
  17.8 5.2 %gauges.1 = (f32[272,640]{1,0:T(8,128)S(1)}, f32[4,272,640]{2,1,0:T(8,128)S(1)}) custom-call(s32[4]{0:T(128)S(1)} %pad_add_fusion.place_ref, s32[2048]{0:T(1024)S(1)} %copy-done.8, s32[2048]{0:T(1024)S(1)} %copy-done.9, f32[4,2048]{1,0:T(4,128)S(1)} %copy-done.7), custom_call_target="tpu_custom_call" | custom-call | tf_op jit(solution)/shard_map/gauges/pallas_call | solution.py:539
  22.9 1.5 %copy-done.1 = f32[4,272,640]{2,1,0:T(8,128)} copy-done((f32[4,272,640]{2,1,0:T(8,128)}, f32[4,272,640]{2,1,0:T(8,128)S(1)}, u32[]{:S(2)}) %copy-start.1) | copy-done | bytes 2785304
  24.5 0.5 copy-done.12
  25.0 21.1 %all-to-all-done = f32[128,4224,1]{1,2,0:T(1,128)S(1)} async-done(((f32[128,4224,1]{1,2,0:T(1,128)}), f32[128,4224,1]{1,2,0:T(1,128)S(1)}, u32[]{:S(2)}, u32[]{:S(2)}) %all-to-all-start) | async-done | bytes 2162720 | tf_op jit(solution)/shard_map/all_to_all | solution.py:523
  46.1 0.7 copy-done.11
  46.8 3.2 %scatter.1 = (f32[256,512]{1,0:T(8,128)S(1)}, f32[32,256]{1,0:T(8,128)S(1)}, f32[32,256]{1,0:T(8,128)S(1)}, f32[32,512]{1,0:T(8,128)S(1)}, f32[32,512]{1,0:T(8,128)S(1)}) custom-call(f32[128,1,4224]{2,1,0:T(1,128)S(1)} %bitcast.14, f32[4224,128]{1,0:T(8,128)S(1)} %bitcast.15, s32[256,512]{1,0:T(8,128)S(1)} %copy-done, ...), custom_call_target="tpu_custom_call" | custom-call | tf_op jit(solution)/shard_map/scatter/pallas_call | solution.py:549
  50.1 1.3 %collective-permute-start = (f32[32,256]{1,0:T(8,128)S(1)}, f32[32,256]{1,0:T(8,128)S(1)}, u32[]{:S(2)}, u32[]{:S(2)}) collective-permute-start(f32[32,256]{1,0:T(8,128)S(1)} %get-tuple-element.29), channel_id=1, source_target_pairs={{1,0},{2,1},{3,2},{4,3},{5,4},{6,5},{7,6},{9,8},{10,9},{11,10},{12... | collective-permute-start | bytes 98312 | tf_op jit(solution)/shard_map/ppermute | solution.py:43
  51.4 4.0 %collective-permute-start.1 = (f32[32,256]{1,0:T(8,128)S(1)}, f32[32,256]{1,0:T(8,128)S(1)}, u32[]{:S(2)}, u32[]{:S(2)}) collective-permute-start(f32[32,256]{1,0:T(8,128)S(1)} %get-tuple-element.30), channel_id=1, source_target_pairs={{0,1},{1,2},{2,3},{3,4},{4,5},{5,6},{6,7},{8,9},{9,10},{10,11},{11... | collective-permute-start | bytes 98312 | tf_op jit(solution)/shard_map/ppermute | solution.py:43
  55.4 1.0 collective-permute-done.1.west_ref
  56.4 0.1 rims.1
  56.5 5.4 %collective-permute-start.2 = (f32[32,640]{1,0:T(8,128)S(1)}, f32[32,640]{1,0:T(8,128)S(1)}, u32[]{:S(2)}, u32[]{:S(2)}) collective-permute-start(f32[32,640]{1,0:T(8,128)S(1)} %get-tuple-element.33), channel_id=1, source_target_pairs={{0,8},{8,16},{16,24},{24,32},{32,40},{40,48},{48,56},{56,64},{64,7... | collective-permute-start | bytes 245768 | tf_op jit(solution)/shard_map/ppermute | solution.py:43
  61.9 1.9 %collective-permute-start.3 = (f32[32,640]{1,0:T(8,128)S(1)}, f32[32,640]{1,0:T(8,128)S(1)}, u32[]{:S(2)}, u32[]{:S(2)}) collective-permute-start(f32[32,640]{1,0:T(8,128)S(1)} %get-tuple-element.34), channel_id=1, source_target_pairs={{8,0},{16,8},{24,16},{32,24},{40,32},{48,40},{56,48},{64,56},{72,6... | collective-permute-start | bytes 245768 | tf_op jit(solution)/shard_map/ppermute | solution.py:43
  63.9 5.3 %collective-permute-done.3.south_ref = f32[32,640]{1,0:T(8,128)S(1)} collective-permute-done((f32[32,640]{1,0:T(8,128)S(1)}, f32[32,640]{1,0:T(8,128)S(1)}, u32[]{:S(2)}, u32[]{:S(2)}) %collective-permute-start.3) | collective-permute-done | bytes 81952 | tf_op jit(solution)/shard_map/ppermute | solution.py:43
  69.2 31.1 %solve.1 = (f32[256,512]{1,0:T(8,128)}, f32[256,512]{1,0:T(8,128)}, f32[128,128]{1,0:T(8,128)}) custom-call(s32[4]{0:T(128)S(1)} %copy-done.13, s32[2048]{0:T(1024)S(1)} %copy-done.8, s32[2048]{0:T(1024)S(1)} %copy-done.9, f32[256,512]{1,0:T(8,128)S(1)} %get-tuple-element.28.eta_ref, f32[256,512]{1,0:T(8,128)S(1)} %copy-done.4, s32[256,512]{1,0:T(8,128)S(1)} %copy-done, ...), custom_call_target="tpu_custom_call" | custom-call | tf_op jit(solution)/shard_map/solve/pallas_call | solution.py:576
  100.3 9.2 %all-to-all-start.1 = ((f32[128,1,128]{2,1,0:T(1,128)}), f32[128,1,128]{2,1,0:T(1,128)S(1)}, u32[]{:S(2)}, u32[]{:S(2)}) async-start(f32[128,1,128]{2,1,0:T(1,128)} %bitcast.8), calls=%async_computation.1 | async-start | bytes 131072 | tf_op jit(solution)/shard_map/all_to_all | solution.py:608
  109.6 0.1 convert_add_fusion
  109.6 0.1 copy.28
  109.7 9.7 %all-to-all-done.1 = f32[128,1,128]{2,1,0:T(1,128)S(1)} async-done(((f32[128,1,128]{2,1,0:T(1,128)}), f32[128,1,128]{2,1,0:T(1,128)S(1)}, u32[]{:S(2)}, u32[]{:S(2)}) %all-to-all-start.1) | async-done | bytes 65568 | tf_op jit(solution)/shard_map/all_to_all | solution.py:608
  119.4 0.1 copy.26
  119.5 0.1 select_reduce_fusion
  119.7 0.5 div.3
  120.2 0.1 copy.27
  120.3 0.8 reshape.41
  (28 shorter events, 0.1 us)
Async XLA Ops:
  4.3 11.6 %copy-start = (s32[256,512]{1,0:T(8,128)S(1)}, s32[256,512]{1,0:T(8,128)}, u32[]{:S(2)}) copy-start(s32[256,512]{1,0:T(8,128)} %wet_ref.5) | copy-start | bytes 1572868
  4.3 11.6 %copy-start.3 = (f32[256,512]{1,0:T(8,128)S(1)}, f32[256,512]{1,0:T(8,128)}, u32[]{:S(2)}) copy-start(f32[256,512]{1,0:T(8,128)} %depth_ref.3) | copy-start | bytes 1572868
  4.3 13.5 %copy-start.7 = (f32[4,2048]{1,0:T(4,128)S(1)}, f32[4,2048]{1,0:T(4,128)}, u32[]{:S(2)}) copy-start(f32[4,2048]{1,0:T(4,128)} %obs_ref.1) | copy-start | bytes 98308
  4.3 13.5 %copy-start.8 = (s32[2048]{0:T(1024)S(1)}, s32[2048]{0:T(1024)}, u32[]{:S(2)}) copy-start(s32[2048]{0:T(1024)} %grow_ref.1) | copy-start | bytes 24580
  4.3 13.4 %copy-start.9 = (s32[2048]{0:T(1024)S(1)}, s32[2048]{0:T(1024)}, u32[]{:S(2)}) copy-start(s32[2048]{0:T(1024)} %gcol_ref.1) | copy-start | bytes 24580
  4.3 41.7 %all-to-all-start = ((f32[128,4224,1]{1,2,0:T(1,128)}), f32[128,4224,1]{1,2,0:T(1,128)S(1)}, u32[]{:S(2)}, u32[]{:S(2)}) async-start(f32[128,4224,1]{1,2,0:T(1,128)} %bitcast.18), calls=%async_computation | async-start | bytes 4325376 | tf_op jit(solution)/shard_map/all_to_all | solution.py:523
  15.8 1.0 copy-start.5
  17.0 0.6 copy-start.10
  22.9 1.5 %copy-start.1 = (f32[4,272,640]{2,1,0:T(8,128)}, f32[4,272,640]{2,1,0:T(8,128)S(1)}, u32[]{:S(2)}) copy-start(f32[4,272,640]{2,1,0:T(8,128)S(1)} %get-tuple-element.35.obs) | copy-start | bytes 8355844
  24.5 0.5 copy-start.12
  46.1 0.7 copy-start.11
  46.8 22.4 %copy-start.2 = (f32[4,272,640]{2,1,0:T(8,128)S(1)}, f32[4,272,640]{2,1,0:T(8,128)}, u32[]{:S(2)}) copy-start(f32[4,272,640]{2,1,0:T(8,128)} %copy-done.1) | copy-start | bytes 8355844
  46.8 22.4 %copy-start.4 = (f32[256,512]{1,0:T(8,128)S(1)}, f32[256,512]{1,0:T(8,128)}, u32[]{:S(2)}) copy-start(f32[256,512]{1,0:T(8,128)} %depth_ref.3) | copy-start | bytes 1572868
  46.8 22.4 %copy-start.6 = (f32[256,512]{1,0:T(8,128)S(1)}, f32[256,512]{1,0:T(8,128)}, u32[]{:S(2)}) copy-start(f32[256,512]{1,0:T(8,128)} %fric_ref.3) | copy-start | bytes 1572868
  46.8 22.4 %copy-start.13 = (s32[4]{0:T(128)S(1)}, s32[4]{0:T(128)}, u32[]{:S(2)}) copy-start(s32[4]{0:T(128)} %copy-done.12) | copy-start | bytes 52
  50.1 5.3 %collective-permute-start = (f32[32,256]{1,0:T(8,128)S(1)}, f32[32,256]{1,0:T(8,128)S(1)}, u32[]{:S(2)}, u32[]{:S(2)}) collective-permute-start(f32[32,256]{1,0:T(8,128)S(1)} %get-tuple-element.29), channel_id=1, source_target_pairs={{1,0},{2,1},{3,2},{4,3},{5,4},{6,5},{7,6},{9,8},{10,9},{11,10},{12... | collective-permute-start | bytes 98312 | tf_op jit(solution)/shard_map/ppermute | solution.py:43
  51.4 5.0 %collective-permute-start.1 = (f32[32,256]{1,0:T(8,128)S(1)}, f32[32,256]{1,0:T(8,128)S(1)}, u32[]{:S(2)}, u32[]{:S(2)}) collective-permute-start(f32[32,256]{1,0:T(8,128)S(1)} %get-tuple-element.30), channel_id=1, source_target_pairs={{0,1},{1,2},{2,3},{3,4},{4,5},{5,6},{6,7},{8,9},{9,10},{10,11},{11... | collective-permute-start | bytes 98312 | tf_op jit(solution)/shard_map/ppermute | solution.py:43
  56.5 7.4 %collective-permute-start.2 = (f32[32,640]{1,0:T(8,128)S(1)}, f32[32,640]{1,0:T(8,128)S(1)}, u32[]{:S(2)}, u32[]{:S(2)}) collective-permute-start(f32[32,640]{1,0:T(8,128)S(1)} %get-tuple-element.33), channel_id=1, source_target_pairs={{0,8},{8,16},{16,24},{24,32},{32,40},{40,48},{48,56},{56,64},{64,7... | collective-permute-start | bytes 245768 | tf_op jit(solution)/shard_map/ppermute | solution.py:43
  61.9 7.3 %collective-permute-start.3 = (f32[32,640]{1,0:T(8,128)S(1)}, f32[32,640]{1,0:T(8,128)S(1)}, u32[]{:S(2)}, u32[]{:S(2)}) collective-permute-start(f32[32,640]{1,0:T(8,128)S(1)} %get-tuple-element.34), channel_id=1, source_target_pairs={{8,0},{16,8},{24,16},{32,24},{40,32},{48,40},{56,48},{64,56},{72,6... | collective-permute-start | bytes 245768 | tf_op jit(solution)/shard_map/ppermute | solution.py:43
  69.2 40.3 %copy-start.14 = (f32[128,128]{1,0:T(8,128)S(1)}, f32[128,128]{1,0:T(8,128)}, u32[]{:S(2)}) copy-start(f32[128,128]{1,0:T(8,128)} %get-tuple-element.39) | copy-start | bytes 196612
  69.2 50.4 %copy-start.15 = (f32[16]{0:T(128)S(1)}, f32[16]{0:T(128)}, u32[]{:S(2)}) copy-start(f32[16]{0:T(128)} %slip_ref.1) | copy-start | bytes 196
  100.3 19.1 %all-to-all-start.1 = ((f32[128,1,128]{2,1,0:T(1,128)}), f32[128,1,128]{2,1,0:T(1,128)S(1)}, u32[]{:S(2)}, u32[]{:S(2)}) async-start(f32[128,1,128]{2,1,0:T(1,128)} %bitcast.8), calls=%async_computation.1 | async-start | bytes 131072 | tf_op jit(solution)/shard_map/all_to_all | solution.py:608
where the time goes:
time: 122 us; the launch traced here: 121 us
  Pallas kernels  43.4 us (36%)
  waiting for transfers between devices  37.1 us (30%)
  starting transfers between devices  33.4 us (27%)
  local copies, waits for them, and re-layouts  5.56 us (5%)
    pallas_call x1, Pallas kernels, body(): pl.pallas_call(solve_kernel, out_shape=[tile, tile, f((devices, 128), F32...  31.1 us
    all_to_all x1, waiting for transfers between devices, body(): lax.all_to_all(packed.reshape(-1), both, split_axis=0, concat_axis=0, til...  21.1 us
    ppermute x4, starting transfers between devices, shifted(): return lax.ppermute(shard, axis, pairs)  12.6 us
    all_to_all x1, starting transfers between devices, body(): lax.all_to_all(packed.reshape(-1), both, split_axis=0, concat_axis=0, til...  11.5 us
    all_to_all x1, waiting for transfers between devices, body(): lax.all_to_all(back, both, split_axis=0, concat_axis=0, tiled=True)  9.71 us
    all_to_all x1, starting transfers between devices, body(): lax.all_to_all(back, both, split_axis=0, concat_axis=0, tiled=True)  9.24 us
    ppermute x4, waiting for transfers between devices, shifted(): return lax.ppermute(shard, axis, pairs)  6.32 us
    pallas_call x1, Pallas kernels, body(): pl.pallas_call(gauge_kernel, out_shape=[grid, f((steps, rows, cols), F32)...  5.16 us
  transfers between devices with their start and end apart: 6, of which 4 were waited for; matrix products, arithmetic and copies ran while one was open for 0% of the time, Pallas kernels for 4%

commit v1 on v0

--- a/solution.py
+++ b/solution.py
@@ -178,7 +178,8 @@
         bottom_ref[at] = ref[rows - 8 : rows, :].astype(F32)
 
 
-def rim_kernel(east_ref, west_ref, top_in, bottom_in, top_ref, bottom_ref):
+def rim_kernel(east_ref, west_ref, top_in, bottom_in, after, top_ref, bottom_ref):
+    del after
     fields = east_ref.shape[0] // 8
     rows = east_ref.shape[1]
     cols = top_in.shape[1]
@@ -201,20 +202,12 @@
             )
 
 
-def assemble(out, n, ref, east_ref, west_ref, north_ref, south_ref):
-    rows, cols = ref.shape
-    at = slice(8 * n, 8 * n + 8)
-    out[0:8, :] = north_ref[at]
-    out[8 : 8 + rows, 0:cols] = ref[...].astype(F32)
-    out[8 : 8 + rows, cols:] = side_block(east_ref[at], west_ref[at])
-    out[8 + rows : 16 + rows, :] = south_ref[at]
-
-
 def row_iota(shape):
     return lax.broadcasted_iota(I32, shape, 0)
 
 
-def gauge_kernel(place_ref, row_ref, col_ref, obs_ref, count_out, obs_out):
+def gauge_kernel(place_ref, row_ref, col_ref, obs_ref, count_out, obs_out, token_out):
+    token_out[...] = jnp.zeros(token_out.shape, F32)
     steps, rows, cols = obs_out.shape
     own_rows = rows - 2 * HALO
     own_cols = cols - 128
@@ -295,24 +288,144 @@
     return tiles[0]
 
 
-def solve_kernel(
-    place_ref, grow_ref, gcol_ref,
-    eta_ref, depth_ref, wet_ref, fric_ref, east_ref, west_ref, north_ref, south_ref,
-    count, obs, recv, meta_hbm,
-    final_ref, adj_ref, back_ref,
-    depth_x, wet, fric_x, dde, dds, rre, rrs, wwe, wws,
-    surf, fe, fs, ae, pe, qe, as_, ps, qs, adj, ce, cs, grads,
-    parts, reads, meta, sem,
+def statics_of(d, w, m, d_next, w_next, m_next):
+    return d + d_next, ROUGH_SCALE * (m + m_next), w * w_next
+
+
+def south_of(here, after):
+    last = row_iota(here.shape) == 7
+    return jnp.where(last, pltpu.roll(after, 7, 0), pltpu.roll(here, 7, 0))
+
+
+def north_of(flux, before):
+    first = row_iota(flux.shape) == 0
+    return jnp.where(first, pltpu.roll(before, 1, 0), pltpu.roll(flux, 1, 0))
+
+
+def rows_at(i):
+    return pl.ds(pl.multiple_of(i * 8, 8), 8)
+
+
+def divergence(east, south, before):
+    return (east - pltpu.roll(east, 1, 1)) + (south - north_of(south, before))
+
+
+def store_face(refs, at, statics, made):
+    flux, _, p, q = made
+    for ref, value in zip(refs, (*statics, flux, p, q)):
+        ref[at] = value
+
+
+def tile_kernel(eta_ref, depth_ref, wet_ref, fric_ref, *out):
+    east, south = out[:6], out[6:]
+    rows, cols = eta_ref.shape
+    fields = (depth_ref, wet_ref, fric_ref, eta_ref)
+    keep = cols - 128
+
+    def eastward(i, c):
+        here = [ref[rows_at(i), :].astype(F32) for ref in fields]
+        there = [pltpu.roll(v, cols - 1, 1)[:, :keep] for v in here]
+        here = [v[:, :keep] for v in here]
+        statics = statics_of(*here[:3], *there[:3])
+        store_face(east, (rows_at(i + 1), slice(0, keep)), statics, face(None, here[3], there[3], *statics))
+        return c
+
+    def southward(i, c):
+        here = [ref[rows_at(i), :].astype(F32) for ref in fields]
+        there = [south_of(v, ref[rows_at(i + 1), :].astype(F32)) for v, ref in zip(here, fields)]
+        statics = statics_of(*here[:3], *there[:3])
+        store_face(south, (rows_at(i + 1), slice(0, cols)), statics, face(None, here[3], there[3], *statics))
+        return c
+
+    lax.fori_loop(0, rows // 8, eastward, 0, unroll=4)
+    lax.fori_loop(0, rows // 8 - 1, southward, 0, unroll=3)
+
+
+def frame_kernel(
+    eta_ref, depth_ref, wet_ref, fric_ref, east_ref, west_ref, dde, rre, wwe, fe, fs, *refs
 ):
+    east, south = refs[:6], refs[6:12]
+    surf0, wet, surf1, fe1, ae1, pe1, qe1 = refs[12:19]
+    sides = refs[19:]
+    rows, cols = eta_ref.shape
+    fields = (depth_ref, wet_ref, fric_ref, eta_ref)
+    blocks = rows // 8
+    for n, side in enumerate(sides):
+        side[...] = side_block(east_ref[8 * n : 8 * n + 8], west_ref[8 * n : 8 * n + 8])
+
+    def frame(i, c):
+        at = rows_at(i)
+        out = rows_at(i + 1)
+        after = rows_at(jnp.minimum(i + 1, blocks - 1))
+        corner = [side[at, :] for side in sides]
+        tail = [ref[at, cols - 128 :].astype(F32) for ref in fields]
+        head = [ref[at, 0:128].astype(F32) for ref in fields]
+        here = [jnp.concatenate(p, axis=1) for p in zip(tail, corner)]
+        there = [
+            pltpu.roll(jnp.concatenate(p, axis=1), 3 * 128 - 1, 1)[:, :256]
+            for p in zip(tail, corner, head)
+        ]
+        statics = statics_of(*here[:3], *there[:3])
+        store_face(east, (out, slice(None)), statics, face(None, here[3], there[3], *statics))
+        there = [south_of(v, side[after, :]) for v, side in zip(corner, sides)]
+        statics = statics_of(*corner[:3], *there[:3])
+        store_face(south, (out, slice(None)), statics, face(None, corner[3], there[3], *statics))
+        for ref, n in ((wet, 1), (surf0, 3)):
+            ref[out, 0:cols] = fields[n][at, :].astype(F32)
+            ref[out, cols:] = corner[n]
+        return c
+
+    lax.fori_loop(0, blocks, frame, 0, unroll=2)
+    cut = cols - 128
+
+    def whole(left, right, at):
+        width = left.shape[1] - right.shape[1]
+        return jnp.concatenate([left[at, 0:width], right[at, :]], axis=1)
+
+    def surface(i, before):
+        at = rows_at(i)
+        flux = whole(fs, south[3], at)
+        div = divergence(whole(fe, east[3], at), flux, before)
+        surf1[at, :] = wet[at, :] * (surf0[at, :] - (mass_gain * PUSH) * div)
+        return flux
+
+    lax.fori_loop(2, blocks, surface, whole(fs, south[3], rows_at(1)), unroll=2)
+
+    def eastward(i, c):
+        at = rows_at(i)
+        s = surf1[at, :]
+        statics = [whole(a, b, at) for a, b in ((dde, east[0]), (rre, east[1]), (wwe, east[2]))]
+        made = face(whole(fe, east[3], at), s, pltpu.roll(s, s.shape[1] - 1, 1), *statics)
+        for ref, value in zip((fe1, ae1, pe1, qe1), made):
+            ref[at, :] = value
+        return c
+
+    lax.fori_loop(2, blocks, eastward, 0, unroll=3)
+
+
+def solve_kernel(*refs):
+    place_ref, grow_ref, gcol_ref = refs[:3]
+    east0, south0, east_part, south_part = (refs[3 + 6 * n : 9 + 6 * n] for n in range(4))
+    surf0, wet, surf1, fe1, ae1, pe1, qe1 = refs[27:34]
+    north_ref, south_ref, top_ref, bottom_ref, count, obs, recv, meta_hbm = refs[34:42]
+    final_ref, adj_ref, back_ref = refs[42:45]
+    (
+        surf_s, ae_s, as_s, pe_s, qe_s, ps_s, qs_s,
+        adj, ce, cs, grads, parts, reads, meta, sem,
+    ) = refs[45:]
     steps, rows, cols = obs.shape
-    own_rows, own_cols = eta_ref.shape
+    own_rows, own_cols = final_ref.shape
+    dde, rre, wwe, fe0, pe0, qe0 = east0
+    dds, rrs, wws, fs, ps0, qs0 = south0
+    surf = [surf0, surf1] + [surf_s.at[n] for n in range(steps - 1)]
+    ae = [None, ae1] + [ae_s.at[n] for n in range(steps - 2)]
+    pe = [pe0, pe1] + [pe_s.at[n] for n in range(steps - 2)]
+    qe = [qe0, qe1] + [qe_s.at[n] for n in range(steps - 2)]
+    as_ = [None] + [as_s.at[n] for n in range(steps - 1)]
+    ps = [ps0] + [ps_s.at[n] for n in range(steps - 1)]
+    qs = [qs0] + [qs_s.at[n] for n in range(steps - 1)]
     load = meta_copy(meta_hbm, meta, sem)
     load.start()
-    halos = (east_ref, west_ref, north_ref, south_ref)
-    assemble(depth_x, 0, depth_ref, *halos)
-    assemble(wet, 1, wet_ref, *halos)
-    assemble(fric_x, 2, fric_ref, *halos)
-    assemble(surf.at[0], 3, eta_ref, *halos)
     sub = row_iota((8, cols))
     last = sub == 7
     firstrow = sub == 0
@@ -322,59 +435,83 @@
     def nxt(i):
         return pl.multiple_of(jnp.minimum(i * 8 + 8, rows - 8), 8)
 
-    for k in range(steps):
+    def take(i, c):
+        at = rows_at(i)
+        for whole, part in zip(east0 + south0, east_part + south_part):
+            whole[at, cols - part.shape[1] :] = part[at, :]
+        return c
+
+    lax.fori_loop(1, blocks - 1, take, 0, unroll=2)
+
+    def field(ref, n):
+        return ref[8 * n : 8 * n + 8, :]
+
+    def edge_face(refs, i, ref, neighbour):
+        here = [field(ref, n) for n in range(4)]
+        there = neighbour(here)
+        statics = statics_of(*here[:3], *there[:3])
+        store_face(refs, (rows_at(i), slice(None)), statics, face(None, here[3], there[3], *statics))
+
+    def east_of(here):
+        return [pltpu.roll(v, cols - 1, 1) for v in here]
+
+    def above(ref):
+        return lambda here: [south_of(v, field(ref, n)) for n, v in enumerate(here)]
+
+    for i, ref in ((0, north_ref), (blocks - 1, south_ref)):
+        surf0[rows_at(i), :] = field(ref, 3)
+        wet[rows_at(i), :] = field(ref, 1)
+        edge_face(east0, i, ref, east_of)
+    edge_face(south0, 0, north_ref, above(top_ref))
+    edge_face(south0, blocks - 2, bottom_ref, above(south_ref))
+    edge_face(south0, blocks - 1, south_ref, above(south_ref))
+    rim = (0, 1, blocks - 2, blocks - 1)
+    for i in rim:
+        at = rows_at(i)
+        before = fs[rows_at(max(i - 1, 0)), :]
+        div = divergence(fe0[at, :], fs[at, :], before)
+        surf1[at, :] = wet[at, :] * (surf0[at, :] - (mass_gain * PUSH) * div)
+
+    for k in range(1, steps):
 
         def eastward(i, c, k=k):
-            here = pl.ds(pl.multiple_of(i * 8, 8), 8)
-            if k == 0:
-                d, w, m = depth_x[here, :], wet[here, :], fric_x[here, :]
-                dde[here, :] = d + pltpu.roll(d, cols - 1, 1)
-                wwe[here, :] = w * pltpu.roll(w, cols - 1, 1)
-                rre[here, :] = ROUGH_SCALE * (m + pltpu.roll(m, cols - 1, 1))
-            s = surf[k, here, :]
-            old = None if k == 0 else fe[here, :]
+            here = rows_at(i)
+            s = surf[k][here, :]
+            old = fe0 if k == 1 else fe1
             flux, a, p, q = face(
-                old, s, pltpu.roll(s, cols - 1, 1), dde[here, :], rre[here, :], wwe[here, :]
+                old[here, :], s, pltpu.roll(s, cols - 1, 1), dde[here, :], rre[here, :], wwe[here, :]
             )
-            fe[here, :] = flux
-            if k > 0:
-                ae[k - 1, here, :] = a
-            pe[k, here, :] = p
-            qe[k, here, :] = q
+            fe1[here, :] = flux
+            ae[k][here, :] = a
+            pe[k][here, :] = p
+            qe[k][here, :] = q
             return c
 
         def southward(i, carry, k=k):
             s, s_up, f_down = carry
-            here = pl.ds(pl.multiple_of(i * 8, 8), 8)
-            after = pl.ds(nxt(i), 8)
-            if k == 0:
-
-                def south(ref):
-                    return jnp.where(last, pltpu.roll(ref[after, :], 7, 0), pltpu.roll(ref[here, :], 7, 0))
-
-                dds[here, :] = depth_x[here, :] + south(depth_x)
-                wws[here, :] = wet[here, :] * south(wet)
-                rrs[here, :] = ROUGH_SCALE * (fric_x[here, :] + south(fric_x))
-            sn = surf[k, after, :]
+            here = rows_at(i)
+            sn = surf[k][pl.ds(nxt(i), 8), :]
             sn_up = pltpu.roll(sn, 7, 0)
-            old = None if k == 0 else fs[here, :]
             flux, a, p, q = face(
-                old, s, jnp.where(last, sn_up, s_up), dds[here, :], rrs[here, :], wws[here, :]
+                fs[here, :], s, jnp.where(last, sn_up, s_up), dds[here, :], rrs[here, :], wws[here, :]
             )
             fs[here, :] = flux
-            if k > 0:
-                as_[k - 1, here, :] = a
-            ps[k, here, :] = p
-            qs[k, here, :] = q
+            as_[k][here, :] = a
+            ps[k][here, :] = p
+            qs[k][here, :] = q
             down = pltpu.roll(flux, 1, 0)
-            east = fe[here, :]
+            east = fe1[here, :]
             div = east - pltpu.roll(east, 1, 1)
             div = div + (flux - jnp.where(firstrow, f_down, down))
-            surf[k + 1, here, :] = wet[here, :] * (s - (mass_gain * PUSH) * div)
+            surf[k + 1][here, :] = wet[here, :] * (s - (mass_gain * PUSH) * div)
             return sn, sn_up, down
 
-        s0 = surf[k, 0:8, :]
-        lax.fori_loop(0, blocks, eastward, 0, unroll=UNROLL)
+        s0 = surf[k][0:8, :]
+        if k == 1:
+            for i in rim:
+                eastward(i, 0)
+        else:
+            lax.fori_loop(0, blocks, eastward, 0, unroll=UNROLL)
         lax.fori_loop(
             0,
             blocks,
@@ -383,7 +520,7 @@
             unroll=UNROLL,
         )
 
-    final_ref[...] = surf[steps, HALO : HALO + own_rows, 0:own_cols]
+    final_ref[...] = surf[steps][HALO : HALO + own_rows, 0:own_cols]
 
     gx, gy = place_ref[0], place_ref[1]
     lane8 = lax.broadcasted_iota(I32, (8, 128), 1)
@@ -402,7 +539,7 @@
             )
             spots.append((at, (sub8 == r % 8) & (lane8 == q % 128)))
         for k in range(steps):
-            picked = [jnp.where(hit, surf[(k + 1,) + at], 0.0) for at, hit in spots]
+            picked = [jnp.where(hit, surf[k + 1][at], 0.0) for at, hit in spots]
             reads[k * per_tile + g0 : k * per_tile + g0 + 8, :] = merge_rows(picked)
     values = jnp.sum(reads[...], axis=1, keepdims=True)
     spots = row_iota(reads.shape) + SLOTS == lax.broadcasted_iota(I32, reads.shape, 1)
@@ -413,7 +550,7 @@
     for k in reversed(range(steps)):
 
         def seeded(value, at, k):
-            seed = count[at, :] * surf[k + 1, at, :] - obs[k, at, :]
+            seed = count[at, :] * surf[k + 1][at, :] - obs[k, at, :]
             return seed if value is None else value + seed
 
         def b_of(r, k=k):
@@ -435,13 +572,13 @@
                 ge = ge + ce[here, :]
                 gs = gs + cs[here, :]
             if k > 0:
-                ce[here, :] = ge * ae[k - 1, here, :]
-                cs[here, :] = gs * as_[k - 1, here, :]
-            xe = ge * pe[k, here, :]
-            xs = gs * ps[k, here, :]
+                ce[here, :] = ge * ae[k][here, :]
+                cs[here, :] = gs * as_[k][here, :]
+            xe = ge * pe[k][here, :]
+            xs = gs * ps[k][here, :]
             down = pltpu.roll(xs, 1, 0)
-            out = b + ge * qe[k, here, :] + pltpu.roll(xe, 1, 1)
-            out = out + gs * qs[k, here, :] + jnp.where(firstrow, x_down, down)
+            out = b + ge * qe[k][here, :] + pltpu.roll(xe, 1, 1)
+            out = out + gs * qs[k][here, :] + jnp.where(firstrow, x_down, down)
             if k > 0:
                 out = seeded(out, here, k - 1)
             adj[here, :] = out
@@ -536,11 +673,11 @@
     place = jnp.stack(
         [lax.axis_index("gx"), lax.axis_index("gy"), jnp.int32(width_x), jnp.int32(width_y)]
     ).astype(I32)
-    count, obs = pl.pallas_call(
+    count, obs, token = pl.pallas_call(
         gauge_kernel,
-        out_shape=[grid, f((steps, rows, cols), F32)],
+        out_shape=[grid, f((steps, rows, cols), F32), f((8, 128), F32)],
         in_specs=[smem()] * 4,
-        out_specs=[vmem()] * 2,
+        out_specs=[vmem()] * 3,
         name="gauges",
         compiler_params=pltpu.CompilerParams(vmem_limit_bytes=2 * MIB),
     )(place, gauge_row, gauge_col, observed)
@@ -557,53 +694,70 @@
         + [pltpu.VMEM((rows_here * cols_here // 1024, 8, 128), F32)] * SLOTS,
         name="scatter",
         compiler_params=pltpu.CompilerParams(vmem_limit_bytes=10 * MIB),
-    )(slots_view, recv, wet_mask, *edges, count)
+    )(slots_view, recv, wet_mask, *edges, token)
     from_east = shifted(west, "gy", -1)
     from_west = shifted(east, "gy", 1)
+    tiles = (eta, ocean_depth, wet_mask, manning)
+    made = pl.pallas_call(
+        tile_kernel,
+        out_shape=[grid] * 12,
+        in_specs=[vmem()] * 4,
+        out_specs=[vmem()] * 12,
+        compiler_params=pltpu.CompilerParams(vmem_limit_bytes=MIB),
+        name="tile",
+    )(*tiles)
     top, bottom = pl.pallas_call(
         rim_kernel,
         out_shape=[f((32, cols), F32)] * 2,
-        in_specs=[vmem()] * 4,
+        in_specs=[vmem()] * 4 + [hbm()],
         out_specs=[vmem()] * 2,
+        compiler_params=pltpu.CompilerParams(vmem_limit_bytes=MIB),
         name="rims",
-        compiler_params=pltpu.CompilerParams(vmem_limit_bytes=2 * MIB),
-    )(from_east, from_west, top, bottom)
+    )(from_east, from_west, top, bottom, made[0])
     from_south = shifted(top, "gx", -1)
     from_north = shifted(bottom, "gx", 1)
+    framed = pl.pallas_call(
+        frame_kernel,
+        out_shape=[f((rows, 256), F32)] * 6 + [f((rows, 128), F32)] * 6 + [grid] * 7,
+        in_specs=[vmem()] * 11,
+        out_specs=[vmem()] * 19,
+        scratch_shapes=[pltpu.VMEM((rows_here, 128), F32)] * 4,
+        compiler_params=pltpu.CompilerParams(vmem_limit_bytes=2 * MIB),
+        name="frame",
+    )(*tiles, from_east, from_west, *made[:4], made[9])
 
     tile = f((rows_here, cols_here), F32)
-    scratch = pltpu.VMEM((rows, cols), F32)
+
+    def many(n):
+        return pltpu.VMEM((n, rows, cols), F32)
+
     final, adjoint, back = pl.pallas_call(
         solve_kernel,
         out_shape=[tile, tile, f((devices, 128), F32)],
-        in_specs=[smem()] * 3 + [vmem()] * 11 + [hbm()],
+        in_specs=[smem()] * 3 + [vmem()] * 38 + [hbm()],
         out_specs=[vmem()] * 3,
-        scratch_shapes=[scratch] * 9
-        + [
-            pltpu.VMEM((steps + 1, rows, cols), F32),
-            scratch,
-            scratch,
-            pltpu.VMEM((steps - 1, rows, cols), F32),
-            pltpu.VMEM((steps, rows, cols), F32),
-            pltpu.VMEM((steps, rows, cols), F32),
-            pltpu.VMEM((steps - 1, rows, cols), F32),
-            pltpu.VMEM((steps, rows, cols), F32),
-            pltpu.VMEM((steps, rows, cols), F32),
-            scratch,
-            scratch,
-            scratch,
+        scratch_shapes=[
+            many(steps - 1),
+            many(steps - 2),
+            many(steps - 1),
+            many(steps - 2),
+            many(steps - 2),
+            many(steps - 1),
+            many(steps - 1),
+            pltpu.VMEM((rows, cols), F32),
+            pltpu.VMEM((rows, cols), F32),
+            pltpu.VMEM((rows, cols), F32),
             pltpu.VMEM((rows // 8 * (cols_here // 128), 8, 128), F32),
             pltpu.VMEM((SLOTS, devices, 128), F32),
             pltpu.VMEM((steps * per_tile, 128), F32),
             pltpu.SMEM((devices, 1, 128), F32),
             pltpu.SemaphoreType.DMA,
         ],
+        compiler_params=pltpu.CompilerParams(vmem_limit_bytes=22 * MIB),
         name="solve",
-        compiler_params=pltpu.CompilerParams(vmem_limit_bytes=44 * MIB),
     )(
-        place, gauge_row, gauge_col,
-        eta, ocean_depth, wet_mask, manning, from_east, from_west, from_north, from_south,
-        count, obs, recv, slots_view,
+        place, gauge_row, gauge_col, *made, *framed,
+        from_north, from_south, top, bottom, count, obs, recv, slots_view,
     )
     returned = lax.all_to_all(back, both, split_axis=0, concat_axis=0, tiled=True)
     readings = (

time: 122 us -> 115 us (0.943)
  waiting for transfers between devices: 37.1 us -> 31.2 us
  Pallas kernels: 43.4 us -> 45 us
  starting transfers between devices: 33.4 us -> 32.1 us
    pallas_call x0 -> x2, Pallas kernels: none -> 7.42 us  [the longest x1 5.12 us: body(): pl.pallas_call(frame_kernel, out_shape=[f((rows, 256), F32)] * 6 + [f((ro...]
    ppermute x4, waiting for transfers between devices: 6.32 us -> 0.18 us  [shifted(): return lax.ppermute(shard, axis, pairs)]
    pallas_call x1, Pallas kernels: 31.1 us -> 25.3 us  [body(): pl.pallas_call(solve_kernel, out_shape=[tile, tile, f((devices, 128), F32...]
    unnamed x32 -> x26, local copies, waits for them, and re-layouts: 4.5 us -> 3.54 us
  transfers between devices with their start and end apart: 6 -> 6, of which waited for: 4 -> 3; matrix products, arithmetic and copies ran while one was open for 0% -> 0% of each run, Pallas kernels for 4% -> 11%
where the time goes in v1:
time: 115 us
  Pallas kernels  45 us (39%)
  starting transfers between devices  32.1 us (28%)
  waiting for transfers between devices  31.2 us (27%)
  local copies, waits for them, and re-layouts  4.59 us (4%)
    pallas_call x1, Pallas kernels, body(): pl.pallas_call(solve_kernel, out_shape=[tile, tile, f((devices, 128), F32...  25.3 us
    all_to_all x1, waiting for transfers between devices, body(): lax.all_to_all(packed.reshape(-1), both, split_axis=0, concat_axis=0, til...  21.3 us
    ppermute x4, starting transfers between devices, shifted(): return lax.ppermute(shard, axis, pairs)  12 us
    all_to_all x1, starting transfers between devices, body(): lax.all_to_all(packed.reshape(-1), both, split_axis=0, concat_axis=0, til...  11.5 us
    all_to_all x1, waiting for transfers between devices, body(): lax.all_to_all(back, both, split_axis=0, concat_axis=0, tiled=True)  9.73 us
    all_to_all x1, starting transfers between devices, body(): lax.all_to_all(back, both, split_axis=0, concat_axis=0, tiled=True)  8.61 us
    pallas_call x1, Pallas kernels, body(): pl.pallas_call(gauge_kernel, out_shape=[grid, f((steps, rows, cols), F32)...  5.17 us
    pallas_call x1, Pallas kernels, body(): pl.pallas_call(frame_kernel, out_shape=[f((rows, 256), F32)] * 6 + [f((ro...  5.12 us
  transfers between devices with their start and end apart: 6, of which 3 were waited for; matrix products, arithmetic and copies ran while one was open for 0% of the time, Pallas kernels for 11%

profile of v1, /device:TPU:1, one launch (start us, length us, event | category | flops | bytes accessed | tf_op | source)
XLA Modules:
  0.0 114.7 jit_solution(18176872358315298224)
XLA Ops:
  0.6 3.6 %pack.1 = (f32[4224,128]{1,0:T(8,128)}, f32[128,128]{1,0:T(8,128)}) custom-call(f32[16]{0:T(128)} %slip_ref.1, s32[1,256]{1,0:T(1,128)} %bitcast.22, s32[1,256]{1,0:T(1,128)} %bitcast.23, f32[256,8,128]{2,1,0:T(8,128)} %pattern_hbm.1), custom_call_target="tpu_custom_call" | custom-call | tf_op jit(solution)/shard_map/pack/pallas_call | solution.py:647
  4.3 0.0 copy-start.8
  4.3 0.0 copy-start.9
  4.3 11.5 %all-to-all-start = ((f32[128,4224,1]{1,2,0:T(1,128)}), f32[128,4224,1]{1,2,0:T(1,128)S(1)}, u32[]{:S(2)}, u32[]{:S(2)}) async-start(f32[128,4224,1]{1,2,0:T(1,128)} %bitcast.18), calls=%async_computation | async-start | bytes 4325376 | tf_op jit(solution)/shard_map/all_to_all | solution.py:660
  15.8 0.0 copy-start.2
  15.8 1.0 copy-done.2
  16.9 0.1 static_edges.1
  17.0 0.1 pad_add_fusion.place_ref.refs_0_
  17.1 0.0 copy-done.10
  17.1 5.2 %gauges.1 = (f32[272,640]{1,0:T(8,128)S(1)}, f32[4,272,640]{2,1,0:T(8,128)S(1)}, f32[8,128]{1,0:T(8,128)S(1)}) custom-call(s32[4]{0:T(128)S(1)} %pad_add_fusion.place_ref.refs_0_, s32[2048]{0:T(1024)S(1)} %copy-done.8, s32[2048]{0:T(1024)S(1)} %copy-done.9, f32[4,2048]{1,0:T(4,128)S(1)} %copy-done.10), custom_call_target="tpu_custom_call" | custom-call | tf_op jit(solution)/shard_map/gauges/pallas_call | solution.py:676
  22.3 1.6 %copy-done.4 = f32[4,272,640]{2,1,0:T(8,128)} copy-done((f32[4,272,640]{2,1,0:T(8,128)}, f32[4,272,640]{2,1,0:T(8,128)S(1)}, u32[]{:S(2)}) %copy-start.4) | copy-done | bytes 2785304
  23.9 0.9 copy-done.6
  24.8 21.3 %all-to-all-done = f32[128,4224,1]{1,2,0:T(1,128)S(1)} async-done(((f32[128,4224,1]{1,2,0:T(1,128)}), f32[128,4224,1]{1,2,0:T(1,128)S(1)}, u32[]{:S(2)}, u32[]{:S(2)}) %all-to-all-start) | async-done | bytes 2162720 | tf_op jit(solution)/shard_map/all_to_all | solution.py:660
  46.1 3.2 %scatter.1 = (f32[256,512]{1,0:T(8,128)S(1)}, f32[32,256]{1,0:T(8,128)S(1)}, f32[32,256]{1,0:T(8,128)S(1)}, f32[32,512]{1,0:T(8,128)S(1)}, f32[32,512]{1,0:T(8,128)S(1)}) custom-call(f32[128,1,4224]{2,1,0:T(1,128)S(1)} %bitcast.14, f32[4224,128]{1,0:T(8,128)S(1)} %bitcast.15, s32[256,512]{1,0:T(8,128)S(1)} %copy-done, ...), custom_call_target="tpu_custom_call" | custom-call | tf_op jit(solution)/shard_map/scatter/pallas_call | solution.py:686
  49.3 1.3 %collective-permute-start = (f32[32,256]{1,0:T(8,128)S(1)}, f32[32,256]{1,0:T(8,128)S(1)}, u32[]{:S(2)}, u32[]{:S(2)}) collective-permute-start(f32[32,256]{1,0:T(8,128)S(1)} %get-tuple-element.73), channel_id=1, source_target_pairs={{1,0},{2,1},{3,2},{4,3},{5,4},{6,5},{7,6},{9,8},{10,9},{11,10},{12... | collective-permute-start | bytes 98312 | tf_op jit(solution)/shard_map/ppermute | solution.py:43
  50.6 4.0 %collective-permute-start.1 = (f32[32,256]{1,0:T(8,128)S(1)}, f32[32,256]{1,0:T(8,128)S(1)}, u32[]{:S(2)}, u32[]{:S(2)}) collective-permute-start(f32[32,256]{1,0:T(8,128)S(1)} %get-tuple-element.74), channel_id=1, source_target_pairs={{0,1},{1,2},{2,3},{3,4},{4,5},{5,6},{6,7},{8,9},{9,10},{10,11},{11... | collective-permute-start | bytes 98312 | tf_op jit(solution)/shard_map/ppermute | solution.py:43
  54.6 2.3 %tile.1 = (f32[272,640]{1,0:T(8,128)S(1)}, f32[272,640]{1,0:T(8,128)S(1)}, f32[272,640]{1,0:T(8,128)S(1)}, f32[272,640]{1,0:T(8,128)S(1)}, f32[272,640]{1,0:T(8,...) custom-call(f32[256,512]{1,0:T(8,128)S(1)} %get-tuple-element.60.eta, ...), custom_call_target="tpu_custom_call" | custom-call | tf_op jit(solution)/shard_map/tile/pallas_call | solution.py:701
  56.9 0.1 rims.1
  57.1 4.8 %collective-permute-start.2 = (f32[32,640]{1,0:T(8,128)S(1)}, f32[32,640]{1,0:T(8,128)S(1)}, u32[]{:S(2)}, u32[]{:S(2)}) collective-permute-start(f32[32,640]{1,0:T(8,128)S(1)} %get-tuple-element.96.refs_37_), channel_id=1, source_target_pairs={{0,8},{8,16},{16,24},{24,32},{32,40},{40,48},{48,56},{56,64},{64,7... | collective-permute-start | bytes 245768 | tf_op jit(solution)/shard_map/ppermute | solution.py:43
  61.9 1.9 %collective-permute-start.3 = (f32[32,640]{1,0:T(8,128)S(1)}, f32[32,640]{1,0:T(8,128)S(1)}, u32[]{:S(2)}, u32[]{:S(2)}) collective-permute-start(f32[32,640]{1,0:T(8,128)S(1)} %get-tuple-element.97.refs_36_), channel_id=1, source_target_pairs={{8,0},{16,8},{24,16},{32,24},{40,32},{48,40},{56,48},{64,56},{72,6... | collective-permute-start | bytes 245768 | tf_op jit(solution)/shard_map/ppermute | solution.py:43
  63.9 5.1 %frame.1 = (f32[272,256]{1,0:T(8,128)S(1)}, f32[272,256]{1,0:T(8,128)S(1)}, f32[272,256]{1,0:T(8,128)S(1)}, f32[272,256]{1,0:T(8,128)S(1)}, f32[272,256]{1,0:T(8...) custom-call(f32[256,512]{1,0:T(8,128)S(1)} %get-tuple-element.60.eta, ...), custom_call_target="tpu_custom_call" | custom-call | tf_op jit(solution)/shard_map/frame/pallas_call | solution.py:719
  69.0 0.2 collective-permute-done.3.refs_35_
  69.2 25.3 %solve.1 = (f32[256,512]{1,0:T(8,128)}, f32[256,512]{1,0:T(8,128)}, f32[128,128]{1,0:T(8,128)}) custom-call(s32[4]{0:T(128)S(1)} %pad_add_fusion.place_ref.refs_0_, s32[2048]{0:T(1024)S(1)} %copy-done.8, s32[2048]{0:T(1024)S(1)} %copy-done.9, f32[272,640]{1,0:T(8,128)S(1)} %get-tuple-element.61.dde.after.refs_3_, ...), custom_call_target="tpu_custom_call" | custom-call | tf_op jit(solution)/shard_map/solve/pallas_call | solution.py:734
  94.5 8.6 %all-to-all-start.1 = ((f32[128,1,128]{2,1,0:T(1,128)}), f32[128,1,128]{2,1,0:T(1,128)S(1)}, u32[]{:S(2)}, u32[]{:S(2)}) async-start(f32[128,1,128]{2,1,0:T(1,128)} %bitcast.8), calls=%async_computation.1 | async-start | bytes 131072 | tf_op jit(solution)/shard_map/all_to_all | solution.py:762
  103.1 0.1 convert_add_fusion
  103.2 0.1 copy.28
  103.3 9.7 %all-to-all-done.1 = f32[128,1,128]{2,1,0:T(1,128)S(1)} async-done(((f32[128,1,128]{2,1,0:T(1,128)}), f32[128,1,128]{2,1,0:T(1,128)S(1)}, u32[]{:S(2)}, u32[]{:S(2)}) %all-to-all-start.1) | async-done | bytes 65568 | tf_op jit(solution)/shard_map/all_to_all | solution.py:762
  113.0 0.1 copy.26
  113.1 0.1 select_reduce_fusion
  113.3 0.5 div.3
  113.8 0.1 copy.27
  113.9 0.8 reshape.41
  (24 shorter events, 0.1 us)
Async XLA Ops:
  4.3 11.6 %copy-start = (s32[256,512]{1,0:T(8,128)S(1)}, s32[256,512]{1,0:T(8,128)}, u32[]{:S(2)}) copy-start(s32[256,512]{1,0:T(8,128)} %wet_ref.7) | copy-start | bytes 1572868
  4.3 11.6 %copy-start.1 = (f32[256,512]{1,0:T(8,128)S(1)}, f32[256,512]{1,0:T(8,128)}, u32[]{:S(2)}) copy-start(f32[256,512]{1,0:T(8,128)} %depth_ref.5) | copy-start | bytes 1572868
  4.3 12.8 %copy-start.8 = (s32[2048]{0:T(1024)S(1)}, s32[2048]{0:T(1024)}, u32[]{:S(2)}) copy-start(s32[2048]{0:T(1024)} %refs_1_.1) | copy-start | bytes 24580
  4.3 12.8 %copy-start.9 = (s32[2048]{0:T(1024)S(1)}, s32[2048]{0:T(1024)}, u32[]{:S(2)}) copy-start(s32[2048]{0:T(1024)} %refs_2_.1) | copy-start | bytes 24580
  4.3 12.8 %copy-start.10 = (f32[4,2048]{1,0:T(4,128)S(1)}, f32[4,2048]{1,0:T(4,128)}, u32[]{:S(2)}) copy-start(f32[4,2048]{1,0:T(4,128)} %obs_ref.1) | copy-start | bytes 98308
  4.3 41.7 %all-to-all-start = ((f32[128,4224,1]{1,2,0:T(1,128)}), f32[128,4224,1]{1,2,0:T(1,128)S(1)}, u32[]{:S(2)}, u32[]{:S(2)}) async-start(f32[128,4224,1]{1,2,0:T(1,128)} %bitcast.18), calls=%async_computation | async-start | bytes 4325376 | tf_op jit(solution)/shard_map/all_to_all | solution.py:660
  15.8 1.0 copy-start.2
  22.3 1.6 %copy-start.4 = (f32[4,272,640]{2,1,0:T(8,128)}, f32[4,272,640]{2,1,0:T(8,128)S(1)}, u32[]{:S(2)}) copy-start(f32[4,272,640]{2,1,0:T(8,128)S(1)} %get-tuple-element.99.refs_39_) | copy-start | bytes 8355844
  23.9 0.9 copy-start.6
  46.1 8.5 %copy-start.3 = (f32[256,512]{1,0:T(8,128)S(1)}, f32[256,512]{1,0:T(8,128)}, u32[]{:S(2)}) copy-start(f32[256,512]{1,0:T(8,128)} %fric_ref.5) | copy-start | bytes 1572868
  49.3 7.6 %collective-permute-start = (f32[32,256]{1,0:T(8,128)S(1)}, f32[32,256]{1,0:T(8,128)S(1)}, u32[]{:S(2)}, u32[]{:S(2)}) collective-permute-start(f32[32,256]{1,0:T(8,128)S(1)} %get-tuple-element.73), channel_id=1, source_target_pairs={{1,0},{2,1},{3,2},{4,3},{5,4},{6,5},{7,6},{9,8},{10,9},{11,10},{12... | collective-permute-start | bytes 98312 | tf_op jit(solution)/shard_map/ppermute | solution.py:43
  50.6 6.3 %collective-permute-start.1 = (f32[32,256]{1,0:T(8,128)S(1)}, f32[32,256]{1,0:T(8,128)S(1)}, u32[]{:S(2)}, u32[]{:S(2)}) collective-permute-start(f32[32,256]{1,0:T(8,128)S(1)} %get-tuple-element.74), channel_id=1, source_target_pairs={{0,1},{1,2},{2,3},{3,4},{4,5},{5,6},{6,7},{8,9},{9,10},{10,11},{11... | collective-permute-start | bytes 98312 | tf_op jit(solution)/shard_map/ppermute | solution.py:43
  57.1 11.9 %collective-permute-start.2 = (f32[32,640]{1,0:T(8,128)S(1)}, f32[32,640]{1,0:T(8,128)S(1)}, u32[]{:S(2)}, u32[]{:S(2)}) collective-permute-start(f32[32,640]{1,0:T(8,128)S(1)} %get-tuple-element.96.refs_37_), channel_id=1, source_target_pairs={{0,8},{8,16},{16,24},{24,32},{32,40},{40,48},{48,56},{56,64},{64,7... | collective-permute-start | bytes 245768 | tf_op jit(solution)/shard_map/ppermute | solution.py:43
  61.9 7.3 %collective-permute-start.3 = (f32[32,640]{1,0:T(8,128)S(1)}, f32[32,640]{1,0:T(8,128)S(1)}, u32[]{:S(2)}, u32[]{:S(2)}) collective-permute-start(f32[32,640]{1,0:T(8,128)S(1)} %get-tuple-element.97.refs_36_), channel_id=1, source_target_pairs={{8,0},{16,8},{24,16},{32,24},{40,32},{48,40},{56,48},{64,56},{72,6... | collective-permute-start | bytes 245768 | tf_op jit(solution)/shard_map/ppermute | solution.py:43
  63.9 5.3 %copy-start.5 = (f32[4,272,640]{2,1,0:T(8,128)S(1)}, f32[4,272,640]{2,1,0:T(8,128)}, u32[]{:S(2)}) copy-start(f32[4,272,640]{2,1,0:T(8,128)} %copy-done.4) | copy-start | bytes 8355844
  63.9 5.3 %copy-start.7 = (f32[272,640]{1,0:T(8,128)S(1)}, f32[272,640]{1,0:T(8,128)}, u32[]{:S(2)}) copy-start(f32[272,640]{1,0:T(8,128)} %copy-done.6) | copy-start | bytes 2088964
  69.2 33.9 %copy-start.11 = (f32[128,128]{1,0:T(8,128)S(1)}, f32[128,128]{1,0:T(8,128)}, u32[]{:S(2)}) copy-start(f32[128,128]{1,0:T(8,128)} %get-tuple-element.103) | copy-start | bytes 196612
  69.2 44.1 %copy-start.12 = (f32[16]{0:T(128)S(1)}, f32[16]{0:T(128)}, u32[]{:S(2)}) copy-start(f32[16]{0:T(128)} %slip_ref.1) | copy-start | bytes 196
  94.5 18.5 %all-to-all-start.1 = ((f32[128,1,128]{2,1,0:T(1,128)}), f32[128,1,128]{2,1,0:T(1,128)S(1)}, u32[]{:S(2)}, u32[]{:S(2)}) async-start(f32[128,1,128]{2,1,0:T(1,128)} %bitcast.8), calls=%async_computation.1 | async-start | bytes 131072 | tf_op jit(solution)/shard_map/all_to_all | solution.py:762

commit v2 on v1

--- a/solution.py
+++ b/solution.py
@@ -21,7 +21,7 @@
 ROUGH_SCALE = 0.5 * abs(PUSH) * 2.0 ** (7.0 / 3.0)
 F32 = jnp.float32
 MIB = 1 << 20
-UNROLL = 4
+GROUP = 8
 I32 = jnp.int32
 
 
@@ -375,7 +375,7 @@
             ref[out, cols:] = corner[n]
         return c
 
-    lax.fori_loop(0, blocks, frame, 0, unroll=2)
+    lax.fori_loop(0, blocks, frame, 0, unroll=4)
     cut = cols - 128
 
     def whole(left, right, at):
@@ -389,7 +389,7 @@
         surf1[at, :] = wet[at, :] * (surf0[at, :] - (mass_gain * PUSH) * div)
         return flux
 
-    lax.fori_loop(2, blocks, surface, whole(fs, south[3], rows_at(1)), unroll=2)
+    lax.fori_loop(2, blocks, surface, whole(fs, south[3], rows_at(1)), unroll=6)
 
     def eastward(i, c):
         at = rows_at(i)
@@ -400,7 +400,7 @@
             ref[at, :] = value
         return c
 
-    lax.fori_loop(2, blocks, eastward, 0, unroll=3)
+    lax.fori_loop(2, blocks, eastward, 0, unroll=6)
 
 
 def solve_kernel(*refs):
@@ -411,7 +411,7 @@
     final_ref, adj_ref, back_ref = refs[42:45]
     (
         surf_s, ae_s, as_s, pe_s, qe_s, ps_s, qs_s,
-        adj, ce, cs, grads, parts, reads, meta, sem,
+        adj, ce, cs, spread, turned, west, xe, xs, grads, parts, reads, meta, sem,
     ) = refs[45:]
     steps, rows, cols = obs.shape
     own_rows, own_cols = final_ref.shape
@@ -472,15 +472,51 @@
         div = divergence(fe0[at, :], fs[at, :], before)
         surf1[at, :] = wet[at, :] * (surf0[at, :] - (mass_gain * PUSH) * div)
 
+    def pipelined(first, end, main, carry, begin, finish):
+        groups = (end - first) // GROUP
+
+        def step(g, carry):
+            base = first + g * GROUP
+            prior = jnp.maximum(base - GROUP, first)
+            held = [begin(prior + u) for u in range(GROUP)]
+            for u in range(GROUP):
+                carry = main(base + u, carry)
+            for u in range(GROUP):
+                finish(prior + u, held[u])
+            return carry
+
+        carry = lax.fori_loop(0, groups, step, carry)
+        done = first + groups * GROUP
+        held = [begin(done - GROUP + u) for u in range(GROUP)]
+        for i in range(done, end):
+            carry = main(i, carry)
+        for u in range(GROUP):
+            finish(done - GROUP + u, held[u])
+        held = [begin(i) for i in range(done, end)]
+        for i in range(done, end):
+            finish(i, held[i - done])
+        return carry
+
+    def rotate_into(src, dst, by):
+        def begin(i):
+            return pltpu.roll(src[rows_at(i), :], by, 1)
+
+        def finish(i, value):
+            dst[rows_at(i), :] = value
+
+        return begin, finish
+
+    def nothing(i, c):
+        return c
+
     for k in range(1, steps):
 
         def eastward(i, c, k=k):
             here = rows_at(i)
             s = surf[k][here, :]
+            s_east = pltpu.roll(s, cols - 1, 1) if k == 1 else turned[here, :]
             old = fe0 if k == 1 else fe1
-            flux, a, p, q = face(
-                old[here, :], s, pltpu.roll(s, cols - 1, 1), dde[here, :], rre[here, :], wwe[here, :]
-            )
+            flux, a, p, q = face(old[here, :], s, s_east, dde[here, :], rre[here, :], wwe[here, :])
             fe1[here, :] = flux
             ae[k][here, :] = a
             pe[k][here, :] = p
@@ -500,25 +536,24 @@
             ps[k][here, :] = p
             qs[k][here, :] = q
             down = pltpu.roll(flux, 1, 0)
-            east = fe1[here, :]
-            div = east - pltpu.roll(east, 1, 1)
+            div = fe1[here, :] - west[here, :]
             div = div + (flux - jnp.where(firstrow, f_down, down))
             surf[k + 1][here, :] = wet[here, :] * (s - (mass_gain * PUSH) * div)
             return sn, sn_up, down
 
-        s0 = surf[k][0:8, :]
+        turn_flux = rotate_into(fe1, west, 1)
         if k == 1:
             for i in rim:
                 eastward(i, 0)
+            pipelined(0, blocks, nothing, 0, *turn_flux)
         else:
-            lax.fori_loop(0, blocks, eastward, 0, unroll=UNROLL)
-        lax.fori_loop(
-            0,
-            blocks,
-            southward,
-            (s0, pltpu.roll(s0, 7, 0), jnp.zeros((8, cols), F32)),
-            unroll=UNROLL,
-        )
+            pipelined(0, blocks, eastward, 0, *turn_flux)
+        s0 = surf[k][0:8, :]
+        start = (s0, pltpu.roll(s0, 7, 0), jnp.zeros((8, cols), F32))
+        if k < steps - 1:
+            pipelined(0, blocks, southward, start, *rotate_into(surf[k + 1], turned, cols - 1))
+        else:
+            lax.fori_loop(0, blocks, southward, start, unroll=GROUP)
 
     final_ref[...] = surf[steps][HALO : HALO + own_rows, 0:own_cols]
 
@@ -547,57 +582,54 @@
 
     load.wait()
 
+    def seed(at, k):
+        return count[at, :] * surf[k + 1][at, :] - obs[k, at, :]
+
+    def begin_adjoint(i, c):
+        at = rows_at(i)
+        spread[at, :] = wet[at, :] * seed(at, steps - 1)
+        return c
+
+    turn_spread = rotate_into(spread, turned, cols - 1)
+    turn_x = rotate_into(xe, west, 1)
+    pipelined(0, blocks, begin_adjoint, 0, *turn_spread)
     for k in reversed(range(steps)):
 
-        def seeded(value, at, k):
-            seed = count[at, :] * surf[k + 1][at, :] - obs[k, at, :]
-            return seed if value is None else value + seed
-
-        def b_of(r, k=k):
-            at = pl.ds(r, 8)
-            a = seeded(None, at, k) if k == steps - 1 else adj[at, :]
-            return wet[at, :] * a
-
-        def backward(i, carry, k=k):
-            b, b_up, x_down = carry
-            r = pl.multiple_of(i * 8, 8)
-            here = pl.ds(r, 8)
-            bn = b_of(nxt(i))
-            bn_up = pltpu.roll(bn, 7, 0)
-            b_south = jnp.where(last, bn_up, b_up)
-            b_east = pltpu.roll(b, cols - 1, 1)
-            ge = (mass_gain * PUSH) * (b_east - b)
-            gs = (mass_gain * PUSH) * (b_south - b)
+        def gather(i, c, k=k):
+            at = rows_at(i)
+            b = spread[at, :]
+            ge = (mass_gain * PUSH) * (turned[at, :] - b)
+            gs = (mass_gain * PUSH) * (south_of(b, spread[pl.ds(nxt(i), 8), :]) - b)
             if k < steps - 1:
-                ge = ge + ce[here, :]
-                gs = gs + cs[here, :]
+                ge = ge + ce[at, :]
+                gs = gs + cs[at, :]
             if k > 0:
-                ce[here, :] = ge * ae[k][here, :]
-                cs[here, :] = gs * as_[k][here, :]
-            xe = ge * pe[k][here, :]
-            xs = gs * ps[k][here, :]
-            down = pltpu.roll(xs, 1, 0)
-            out = b + ge * qe[k][here, :] + pltpu.roll(xe, 1, 1)
-            out = out + gs * qs[k][here, :] + jnp.where(firstrow, x_down, down)
+                ce[at, :] = ge * ae[k][at, :]
+                cs[at, :] = gs * as_[k][at, :]
+            xe[at, :] = ge * pe[k][at, :]
+            xs[at, :] = gs * ps[k][at, :]
+            adj[at, :] = (b + ge * qe[k][at, :]) + gs * qs[k][at, :]
+            return c
+
+        def collect(i, c, k=k):
+            at = rows_at(i)
+            before = xs[pl.ds(pl.multiple_of(jnp.maximum(i * 8 - 8, 0), 8), 8), :]
+            out = (adj[at, :] + west[at, :]) + north_of(xs[at, :], before)
             if k > 0:
-                out = seeded(out, here, k - 1)
-            adj[here, :] = out
-            if k == 0:
-                scaled = out * wet[here, :]
+                spread[at, :] = wet[at, :] * (out + seed(at, k - 1))
+            else:
+                out = out[:, 0:own_cols]
+                adj_ref[rows_at(i - HALO // 8), :] = out
+                scaled = out * wet[at, 0:own_cols]
                 for q in range(across):
-                    grads[i * across + q] = scaled[:, q * 128 : q * 128 + 128]
-            return bn, bn_up, down
-
-        b0 = b_of(0)
-        lax.fori_loop(
-            0,
-            blocks,
-            backward,
-            (b0, pltpu.roll(b0, 7, 0), jnp.zeros((8, cols), F32)),
-            unroll=2,
-        )
-
-    adj_ref[...] = adj[HALO : HALO + own_rows, 0:own_cols]
+                    grads[(i - HALO // 8) * across + q] = scaled[:, q * 128 : q * 128 + 128]
+            return c
+
+        pipelined(0, blocks, gather, 0, *turn_x)
+        if k > 0:
+            pipelined(0, blocks, collect, 0, *turn_spread)
+        else:
+            lax.fori_loop(HALO // 8, blocks - HALO // 8, collect, 0, unroll=GROUP)
 
     tiles = recv.shape[0] // CHUNK
 
@@ -606,7 +638,7 @@
             products = []
             for u in range(8):
                 t = i * 8 + u
-                b = meta[t, 0, j].astype(I32) + HALO // 8 * across
+                b = meta[t, 0, j].astype(I32)
                 products.append(grads[b] * recv[pl.ds(t * CHUNK + 8 * j, 8), :])
             parts[j, pl.ds(pl.multiple_of(i * 8, 8), 8), :] = merge_rows(products)
         return c
@@ -744,16 +776,14 @@
             many(steps - 2),
             many(steps - 1),
             many(steps - 1),
-            pltpu.VMEM((rows, cols), F32),
-            pltpu.VMEM((rows, cols), F32),
-            pltpu.VMEM((rows, cols), F32),
-            pltpu.VMEM((rows // 8 * (cols_here // 128), 8, 128), F32),
+            *[pltpu.VMEM((rows, cols), F32)] * 8,
+            pltpu.VMEM((rows_here // 8 * (cols_here // 128), 8, 128), F32),
             pltpu.VMEM((SLOTS, devices, 128), F32),
             pltpu.VMEM((steps * per_tile, 128), F32),
             pltpu.SMEM((devices, 1, 128), F32),
             pltpu.SemaphoreType.DMA,
         ],
-        compiler_params=pltpu.CompilerParams(vmem_limit_bytes=22 * MIB),
+        compiler_params=pltpu.CompilerParams(vmem_limit_bytes=26 * MIB),
         name="solve",
     )(
         place, gauge_row, gauge_col, *made, *framed,

time: 115 us -> 110 us (0.957)
  Pallas kernels: 45 us -> 38.1 us
  waiting for transfers between devices: 31.2 us -> 33.2 us
    pallas_call x1, Pallas kernels: 25.3 us -> 20.4 us  [body(): pl.pallas_call(solve_kernel, out_shape=[tile, tile, f((devices, 128), F32...]
    pallas_call x1, Pallas kernels: 5.12 us -> 3.14 us  [body(): pl.pallas_call(frame_kernel, out_shape=[f((rows, 256), F32)] * 6 + [f((ro...]
    ppermute x4, waiting for transfers between devices: 0.18 us -> 2.17 us  [shifted(): return lax.ppermute(shard, axis, pairs)]
  transfers between devices with their start and end apart: 6 -> 6, of which waited for: 3 -> 3; matrix products, arithmetic and copies ran while one was open for 0% -> 0% of each run, Pallas kernels for 11% -> 10%
where the time goes in v2:
time: 110 us
  Pallas kernels  38.1 us (35%)
  waiting for transfers between devices  33.2 us (30%)
  starting transfers between devices  32 us (29%)
  local copies, waits for them, and re-layouts  4.59 us (4%)
    all_to_all x1, waiting for transfers between devices, body(): lax.all_to_all(packed.reshape(-1), both, split_axis=0, concat_axis=0, til...  21.3 us
    pallas_call x1, Pallas kernels, body(): pl.pallas_call(solve_kernel, out_shape=[tile, tile, f((devices, 128), F32...  20.4 us
    ppermute x4, starting transfers between devices, shifted(): return lax.ppermute(shard, axis, pairs)  12 us
    all_to_all x1, starting transfers between devices, body(): lax.all_to_all(packed.reshape(-1), both, split_axis=0, concat_axis=0, til...  11.5 us
    all_to_all x1, waiting for transfers between devices, body(): lax.all_to_all(back, both, split_axis=0, concat_axis=0, tiled=True)  9.73 us
    all_to_all x1, starting transfers between devices, body(): lax.all_to_all(back, both, split_axis=0, concat_axis=0, tiled=True)  8.49 us
    pallas_call x1, Pallas kernels, body(): pl.pallas_call(gauge_kernel, out_shape=[grid, f((steps, rows, cols), F32)...  5.17 us
    pallas_call x1, Pallas kernels, body(): pl.pallas_call(pack_kernel, out_shape=[f((devices * CHUNK, 128), F32), f(...  3.61 us
  transfers between devices with their start and end apart: 6, of which 3 were waited for; matrix products, arithmetic and copies ran while one was open for 0% of the time, Pallas kernels for 10%

profile of v2, /device:TPU:1, one launch (start us, length us, event | category | flops | bytes accessed | tf_op | source)
XLA Modules:
  0.0 109.6 jit_solution(10433814619893282010)
XLA Ops:
  0.6 3.6 %pack.1 = (f32[4224,128]{1,0:T(8,128)}, f32[128,128]{1,0:T(8,128)}) custom-call(f32[16]{0:T(128)} %slip_ref.1, s32[1,256]{1,0:T(1,128)} %bitcast.22, s32[1,256]{1,0:T(1,128)} %bitcast.23, f32[256,8,128]{2,1,0:T(8,128)} %pattern_hbm.1), custom_call_target="tpu_custom_call" | custom-call | tf_op jit(solution)/shard_map/pack/pallas_call | solution.py:679
  4.3 0.0 copy-start.8
  4.3 0.0 copy-start.9
  4.3 11.5 %all-to-all-start = ((f32[128,4224,1]{1,2,0:T(1,128)}), f32[128,4224,1]{1,2,0:T(1,128)S(1)}, u32[]{:S(2)}, u32[]{:S(2)}) async-start(f32[128,4224,1]{1,2,0:T(1,128)} %bitcast.18), calls=%async_computation | async-start | bytes 4325376 | tf_op jit(solution)/shard_map/all_to_all | solution.py:692
  15.8 0.0 copy-start.2
  15.8 1.0 copy-done.2
  16.9 0.1 static_edges.1
  17.0 0.1 pad_add_fusion.place_ref.refs_0_
  17.1 0.0 copy-done.10
  17.1 5.2 %gauges.1 = (f32[272,640]{1,0:T(8,128)S(1)}, f32[4,272,640]{2,1,0:T(8,128)S(1)}, f32[8,128]{1,0:T(8,128)S(1)}) custom-call(s32[4]{0:T(128)S(1)} %pad_add_fusion.place_ref.refs_0_, s32[2048]{0:T(1024)S(1)} %copy-done.8, s32[2048]{0:T(1024)S(1)} %copy-done.9, f32[4,2048]{1,0:T(4,128)S(1)} %copy-done.10), custom_call_target="tpu_custom_call" | custom-call | tf_op jit(solution)/shard_map/gauges/pallas_call | solution.py:708
  22.3 1.6 %copy-done.4 = f32[4,272,640]{2,1,0:T(8,128)} copy-done((f32[4,272,640]{2,1,0:T(8,128)}, f32[4,272,640]{2,1,0:T(8,128)S(1)}, u32[]{:S(2)}) %copy-start.4) | copy-done | bytes 2785304
  23.9 0.9 copy-done.6
  24.8 21.3 %all-to-all-done = f32[128,4224,1]{1,2,0:T(1,128)S(1)} async-done(((f32[128,4224,1]{1,2,0:T(1,128)}), f32[128,4224,1]{1,2,0:T(1,128)S(1)}, u32[]{:S(2)}, u32[]{:S(2)}) %all-to-all-start) | async-done | bytes 2162720 | tf_op jit(solution)/shard_map/all_to_all | solution.py:692
  46.1 3.2 %scatter.1 = (f32[256,512]{1,0:T(8,128)S(1)}, f32[32,256]{1,0:T(8,128)S(1)}, f32[32,256]{1,0:T(8,128)S(1)}, f32[32,512]{1,0:T(8,128)S(1)}, f32[32,512]{1,0:T(8,128)S(1)}) custom-call(f32[128,1,4224]{2,1,0:T(1,128)S(1)} %bitcast.14, f32[4224,128]{1,0:T(8,128)S(1)} %bitcast.15, s32[256,512]{1,0:T(8,128)S(1)} %copy-done, ...), custom_call_target="tpu_custom_call" | custom-call | tf_op jit(solution)/shard_map/scatter/pallas_call | solution.py:718
  49.3 1.3 %collective-permute-start = (f32[32,256]{1,0:T(8,128)S(1)}, f32[32,256]{1,0:T(8,128)S(1)}, u32[]{:S(2)}, u32[]{:S(2)}) collective-permute-start(f32[32,256]{1,0:T(8,128)S(1)} %get-tuple-element.73), channel_id=1, source_target_pairs={{1,0},{2,1},{3,2},{4,3},{5,4},{6,5},{7,6},{9,8},{10,9},{11,10},{12... | collective-permute-start | bytes 98312 | tf_op jit(solution)/shard_map/ppermute | solution.py:43
  50.6 4.0 %collective-permute-start.1 = (f32[32,256]{1,0:T(8,128)S(1)}, f32[32,256]{1,0:T(8,128)S(1)}, u32[]{:S(2)}, u32[]{:S(2)}) collective-permute-start(f32[32,256]{1,0:T(8,128)S(1)} %get-tuple-element.74), channel_id=1, source_target_pairs={{0,1},{1,2},{2,3},{3,4},{4,5},{5,6},{6,7},{8,9},{9,10},{10,11},{11... | collective-permute-start | bytes 98312 | tf_op jit(solution)/shard_map/ppermute | solution.py:43
  54.6 2.3 %tile.1 = (f32[272,640]{1,0:T(8,128)S(1)}, f32[272,640]{1,0:T(8,128)S(1)}, f32[272,640]{1,0:T(8,128)S(1)}, f32[272,640]{1,0:T(8,128)S(1)}, f32[272,640]{1,0:T(8,...) custom-call(f32[256,512]{1,0:T(8,128)S(1)} %get-tuple-element.60.eta, ...), custom_call_target="tpu_custom_call" | custom-call | tf_op jit(solution)/shard_map/tile/pallas_call | solution.py:733
  56.9 0.1 rims.1
  57.1 4.8 %collective-permute-start.2 = (f32[32,640]{1,0:T(8,128)S(1)}, f32[32,640]{1,0:T(8,128)S(1)}, u32[]{:S(2)}, u32[]{:S(2)}) collective-permute-start(f32[32,640]{1,0:T(8,128)S(1)} %get-tuple-element.96.refs_37_), channel_id=1, source_target_pairs={{0,8},{8,16},{16,24},{24,32},{32,40},{40,48},{48,56},{56,64},{64,7... | collective-permute-start | bytes 245768 | tf_op jit(solution)/shard_map/ppermute | solution.py:43
  61.9 1.9 %collective-permute-start.3 = (f32[32,640]{1,0:T(8,128)S(1)}, f32[32,640]{1,0:T(8,128)S(1)}, u32[]{:S(2)}, u32[]{:S(2)}) collective-permute-start(f32[32,640]{1,0:T(8,128)S(1)} %get-tuple-element.97.refs_36_), channel_id=1, source_target_pairs={{8,0},{16,8},{24,16},{32,24},{40,32},{48,40},{56,48},{64,56},{72,6... | collective-permute-start | bytes 245768 | tf_op jit(solution)/shard_map/ppermute | solution.py:43
  63.9 3.1 %frame.1 = (f32[272,256]{1,0:T(8,128)S(1)}, f32[272,256]{1,0:T(8,128)S(1)}, f32[272,256]{1,0:T(8,128)S(1)}, f32[272,256]{1,0:T(8,128)S(1)}, f32[272,256]{1,0:T(8...) custom-call(f32[256,512]{1,0:T(8,128)S(1)} %get-tuple-element.60.eta, ...), custom_call_target="tpu_custom_call" | custom-call | tf_op jit(solution)/shard_map/frame/pallas_call | solution.py:751
  67.0 2.2 %collective-permute-done.3.refs_35_ = f32[32,640]{1,0:T(8,128)S(1)} collective-permute-done((f32[32,640]{1,0:T(8,128)S(1)}, f32[32,640]{1,0:T(8,128)S(1)}, u32[]{:S(2)}, u32[]{:S(2)}) %collective-permute-start.3) | collective-permute-done | bytes 81952 | tf_op jit(solution)/shard_map/ppermute | solution.py:43
  69.2 20.4 %solve.1 = (f32[256,512]{1,0:T(8,128)}, f32[256,512]{1,0:T(8,128)}, f32[128,128]{1,0:T(8,128)}) custom-call(s32[4]{0:T(128)S(1)} %pad_add_fusion.place_ref.refs_0_, s32[2048]{0:T(1024)S(1)} %copy-done.8, s32[2048]{0:T(1024)S(1)} %copy-done.9, f32[272,640]{1,0:T(8,128)S(1)} %get-tuple-element.61.dde.after.refs_3_, ...), custom_call_target="tpu_custom_call" | custom-call | tf_op jit(solution)/shard_map/solve/pallas_call | solution.py:766
  89.6 8.5 %all-to-all-start.1 = ((f32[128,1,128]{2,1,0:T(1,128)}), f32[128,1,128]{2,1,0:T(1,128)S(1)}, u32[]{:S(2)}, u32[]{:S(2)}) async-start(f32[128,1,128]{2,1,0:T(1,128)} %bitcast.8), calls=%async_computation.1 | async-start | bytes 131072 | tf_op jit(solution)/shard_map/all_to_all | solution.py:792
  98.1 0.1 convert_add_fusion
  98.2 0.1 copy.28
  98.2 9.7 %all-to-all-done.1 = f32[128,1,128]{2,1,0:T(1,128)S(1)} async-done(((f32[128,1,128]{2,1,0:T(1,128)}), f32[128,1,128]{2,1,0:T(1,128)S(1)}, u32[]{:S(2)}, u32[]{:S(2)}) %all-to-all-start.1) | async-done | bytes 65568 | tf_op jit(solution)/shard_map/all_to_all | solution.py:792
  108.0 0.1 copy.26
  108.1 0.1 select_reduce_fusion
  108.2 0.5 div.3
  108.7 0.1 copy.27
  108.9 0.8 reshape.41
  (24 shorter events, 0.1 us)
Async XLA Ops:
  4.3 11.6 %copy-start = (s32[256,512]{1,0:T(8,128)S(1)}, s32[256,512]{1,0:T(8,128)}, u32[]{:S(2)}) copy-start(s32[256,512]{1,0:T(8,128)} %wet_ref.7) | copy-start | bytes 1572868
  4.3 11.6 %copy-start.1 = (f32[256,512]{1,0:T(8,128)S(1)}, f32[256,512]{1,0:T(8,128)}, u32[]{:S(2)}) copy-start(f32[256,512]{1,0:T(8,128)} %depth_ref.5) | copy-start | bytes 1572868
  4.3 12.8 %copy-start.8 = (s32[2048]{0:T(1024)S(1)}, s32[2048]{0:T(1024)}, u32[]{:S(2)}) copy-start(s32[2048]{0:T(1024)} %refs_1_.1) | copy-start | bytes 24580
  4.3 12.8 %copy-start.9 = (s32[2048]{0:T(1024)S(1)}, s32[2048]{0:T(1024)}, u32[]{:S(2)}) copy-start(s32[2048]{0:T(1024)} %refs_2_.1) | copy-start | bytes 24580
  4.3 12.8 %copy-start.10 = (f32[4,2048]{1,0:T(4,128)S(1)}, f32[4,2048]{1,0:T(4,128)}, u32[]{:S(2)}) copy-start(f32[4,2048]{1,0:T(4,128)} %obs_ref.1) | copy-start | bytes 98308
  4.3 41.7 %all-to-all-start = ((f32[128,4224,1]{1,2,0:T(1,128)}), f32[128,4224,1]{1,2,0:T(1,128)S(1)}, u32[]{:S(2)}, u32[]{:S(2)}) async-start(f32[128,4224,1]{1,2,0:T(1,128)} %bitcast.18), calls=%async_computation | async-start | bytes 4325376 | tf_op jit(solution)/shard_map/all_to_all | solution.py:692
  15.8 1.0 copy-start.2
  22.3 1.6 %copy-start.4 = (f32[4,272,640]{2,1,0:T(8,128)}, f32[4,272,640]{2,1,0:T(8,128)S(1)}, u32[]{:S(2)}) copy-start(f32[4,272,640]{2,1,0:T(8,128)S(1)} %get-tuple-element.99.refs_39_) | copy-start | bytes 8355844
  23.9 0.9 copy-start.6
  46.1 8.5 %copy-start.3 = (f32[256,512]{1,0:T(8,128)S(1)}, f32[256,512]{1,0:T(8,128)}, u32[]{:S(2)}) copy-start(f32[256,512]{1,0:T(8,128)} %fric_ref.5) | copy-start | bytes 1572868
  49.3 7.6 %collective-permute-start = (f32[32,256]{1,0:T(8,128)S(1)}, f32[32,256]{1,0:T(8,128)S(1)}, u32[]{:S(2)}, u32[]{:S(2)}) collective-permute-start(f32[32,256]{1,0:T(8,128)S(1)} %get-tuple-element.73), channel_id=1, source_target_pairs={{1,0},{2,1},{3,2},{4,3},{5,4},{6,5},{7,6},{9,8},{10,9},{11,10},{12... | collective-permute-start | bytes 98312 | tf_op jit(solution)/shard_map/ppermute | solution.py:43
  50.6 6.3 %collective-permute-start.1 = (f32[32,256]{1,0:T(8,128)S(1)}, f32[32,256]{1,0:T(8,128)S(1)}, u32[]{:S(2)}, u32[]{:S(2)}) collective-permute-start(f32[32,256]{1,0:T(8,128)S(1)} %get-tuple-element.74), channel_id=1, source_target_pairs={{0,1},{1,2},{2,3},{3,4},{4,5},{5,6},{6,7},{8,9},{9,10},{10,11},{11... | collective-permute-start | bytes 98312 | tf_op jit(solution)/shard_map/ppermute | solution.py:43
  57.1 10.0 %collective-permute-start.2 = (f32[32,640]{1,0:T(8,128)S(1)}, f32[32,640]{1,0:T(8,128)S(1)}, u32[]{:S(2)}, u32[]{:S(2)}) collective-permute-start(f32[32,640]{1,0:T(8,128)S(1)} %get-tuple-element.96.refs_37_), channel_id=1, source_target_pairs={{0,8},{8,16},{16,24},{24,32},{32,40},{40,48},{48,56},{56,64},{64,7... | collective-permute-start | bytes 245768 | tf_op jit(solution)/shard_map/ppermute | solution.py:43
  61.9 7.3 %collective-permute-start.3 = (f32[32,640]{1,0:T(8,128)S(1)}, f32[32,640]{1,0:T(8,128)S(1)}, u32[]{:S(2)}, u32[]{:S(2)}) collective-permute-start(f32[32,640]{1,0:T(8,128)S(1)} %get-tuple-element.97.refs_36_), channel_id=1, source_target_pairs={{8,0},{16,8},{24,16},{32,24},{40,32},{48,40},{56,48},{64,56},{72,6... | collective-permute-start | bytes 245768 | tf_op jit(solution)/shard_map/ppermute | solution.py:43
  63.9 5.3 %copy-start.5 = (f32[4,272,640]{2,1,0:T(8,128)S(1)}, f32[4,272,640]{2,1,0:T(8,128)}, u32[]{:S(2)}) copy-start(f32[4,272,640]{2,1,0:T(8,128)} %copy-done.4) | copy-start | bytes 8355844
  63.9 5.3 %copy-start.7 = (f32[272,640]{1,0:T(8,128)S(1)}, f32[272,640]{1,0:T(8,128)}, u32[]{:S(2)}) copy-start(f32[272,640]{1,0:T(8,128)} %copy-done.6) | copy-start | bytes 2088964
  69.2 28.9 %copy-start.11 = (f32[128,128]{1,0:T(8,128)S(1)}, f32[128,128]{1,0:T(8,128)}, u32[]{:S(2)}) copy-start(f32[128,128]{1,0:T(8,128)} %get-tuple-element.103) | copy-start | bytes 196612
  69.2 39.0 %copy-start.12 = (f32[16]{0:T(128)S(1)}, f32[16]{0:T(128)}, u32[]{:S(2)}) copy-start(f32[16]{0:T(128)} %slip_ref.1) | copy-start | bytes 196
  89.6 18.4 %all-to-all-start.1 = ((f32[128,1,128]{2,1,0:T(1,128)}), f32[128,1,128]{2,1,0:T(1,128)S(1)}, u32[]{:S(2)}, u32[]{:S(2)}) async-start(f32[128,1,128]{2,1,0:T(1,128)} %bitcast.8), calls=%async_computation.1 | async-start | bytes 131072 | tf_op jit(solution)/shard_map/all_to_all | solution.py:792

commit v3 on v2

--- a/solution.py
+++ b/solution.py
@@ -110,18 +110,16 @@
     return jnp.concatenate([east, gap, west], axis=0).T
 
 
-def meta_copy(meta_hbm, meta, sem):
-    return pltpu.make_async_copy(meta_hbm.at[:, :, pl.ds(8 * SLOTS * 128, 128)], meta, sem)
-
-
 def scatter_kernel(
-    meta_hbm, recv_ref, wet_ref, west_in, east_in, top_in, bottom_in, after,
-    eta_ref, west_ref, east_ref, top_ref, bottom_ref, meta, sem, *acc,
+    recv_ref, wet_ref, west_in, east_in, top_in, bottom_in, after,
+    eta_ref, west_ref, east_ref, top_ref, bottom_ref, block_out, block_s, sem, *acc,
 ):
     del after
-    load = meta_copy(meta_hbm, meta, sem)
+    tiles = recv_ref.shape[0] // CHUNK
+    facts = recv_ref[pl.ds(8 * SLOTS, tiles, stride=CHUNK), :]
+    block_out[...] = facts.T[0:8].astype(I32)
+    load = pltpu.make_async_copy(block_out, block_s, sem)
     load.start()
-    tiles = recv_ref.shape[0] // CHUNK
     rows, cols = eta_ref.shape
     across = cols // 128
     zero = jnp.zeros((8, 128), F32)
@@ -142,7 +140,7 @@
         base = pl.multiple_of(i * (8 * CHUNK), 8)
         for u in range(8):
             for j in range(SLOTS):
-                b = meta[i * 8 + u, 0, j].astype(I32)
+                b = block_s[j, i * 8 + u]
                 acc[j][b] = acc[j][b] + recv_ref[pl.ds(base + (u * CHUNK + 8 * j), 8), :]
         return c
 
@@ -407,25 +405,27 @@
     place_ref, grow_ref, gcol_ref = refs[:3]
     east0, south0, east_part, south_part = (refs[3 + 6 * n : 9 + 6 * n] for n in range(4))
     surf0, wet, surf1, fe1, ae1, pe1, qe1 = refs[27:34]
-    north_ref, south_ref, top_ref, bottom_ref, count, obs, recv, meta_hbm = refs[34:42]
+    north_ref, south_ref, top_ref, bottom_ref, count, obs, recv, block_ref = refs[34:42]
     final_ref, adj_ref, back_ref = refs[42:45]
-    (
-        surf_s, ae_s, as_s, pe_s, qe_s, ps_s, qs_s,
-        adj, ce, cs, spread, turned, west, xe, xs, grads, parts, reads, meta, sem,
-    ) = refs[45:]
     steps, rows, cols = obs.shape
+    scratch = list(refs[45:])
+
+    def take_scratch(n):
+        taken = scratch[:n]
+        del scratch[:n]
+        return taken
+
+    surf = [surf0, surf1] + take_scratch(steps - 1)
+    ae = [None, ae1] + take_scratch(steps - 2)
     own_rows, own_cols = final_ref.shape
     dde, rre, wwe, fe0, pe0, qe0 = east0
     dds, rrs, wws, fs, ps0, qs0 = south0
-    surf = [surf0, surf1] + [surf_s.at[n] for n in range(steps - 1)]
-    ae = [None, ae1] + [ae_s.at[n] for n in range(steps - 2)]
-    pe = [pe0, pe1] + [pe_s.at[n] for n in range(steps - 2)]
-    qe = [qe0, qe1] + [qe_s.at[n] for n in range(steps - 2)]
-    as_ = [None] + [as_s.at[n] for n in range(steps - 1)]
-    ps = [ps0] + [ps_s.at[n] for n in range(steps - 1)]
-    qs = [qs0] + [qs_s.at[n] for n in range(steps - 1)]
-    load = meta_copy(meta_hbm, meta, sem)
-    load.start()
+    as_ = [None] + take_scratch(steps - 1)
+    pe = [pe0, pe1] + take_scratch(steps - 2)
+    qe = [qe0, qe1] + take_scratch(steps - 2)
+    ps = [ps0] + take_scratch(steps - 1)
+    qs = [qs0] + take_scratch(steps - 1)
+    adj, ce, cs, spread, turned, west, xe, xs, grads, parts, reads = scratch
     sub = row_iota((8, cols))
     last = sub == 7
     firstrow = sub == 0
@@ -580,8 +580,6 @@
     spots = row_iota(reads.shape) + SLOTS == lax.broadcasted_iota(I32, reads.shape, 1)
     reading_row = jnp.sum(jnp.where(spots, values, 0.0), axis=0, keepdims=True)
 
-    load.wait()
-
     def seed(at, k):
         return count[at, :] * surf[k + 1][at, :] - obs[k, at, :]
 
@@ -638,7 +636,7 @@
             products = []
             for u in range(8):
                 t = i * 8 + u
-                b = meta[t, 0, j].astype(I32)
+                b = block_ref[j, t]
                 products.append(grads[b] * recv[pl.ds(t * CHUNK + 8 * j, 8), :])
             parts[j, pl.ds(pl.multiple_of(i * 8, 8), 8), :] = merge_rows(products)
         return c
@@ -649,6 +647,42 @@
     for j in range(SLOTS):
         out = jnp.where(lanes == j, jnp.sum(parts[j], axis=1, keepdims=True), out)
     back_ref[...] = out
+
+
+def closing_kernel(back_ref, table_ref, slip_ref, readings_ref, grad_ref):
+    tiles = back_ref.shape[0]
+    steps, gauges = readings_ref.shape
+    faults = grad_ref.shape[0]
+    per = gauges // tiles
+    width = 128 // per
+    lane = lax.broadcasted_iota(I32, (8, 128), 1)
+    sub = row_iota((8, 128))
+
+    turned = [
+        pltpu.roll(back_ref[8 * c : 8 * c + 8, :], 0, 1, stride=per, stride_axis=0)
+        for c in range(tiles // width)
+    ]
+    for k in range(steps):
+        keep = (lane + 128 - SLOTS) % 128 // per == (sub + k) % width
+        for c0 in range(0, tiles // width, 8):
+            rows = merge_rows([jnp.where(keep, v, 0.0) for v in turned[c0 : c0 + 8]])
+            rows = pltpu.roll(rows, 128 - SLOTS - per * k, 1)
+            for c in range(8):
+                at = slice((c0 + c) * 128, (c0 + c + 1) * 128)
+                readings_ref[k : k + 1, at] = rows[c : c + 1, :]
+
+    totals = [jnp.zeros((8, 128), F32)] * faults
+    for c in range(tiles // 8):
+        fault = pltpu.roll(table_ref[8 * c : 8 * c + 8, :], 128 - 8, 1)
+        value = jnp.where(lane < SLOTS, back_ref[8 * c : 8 * c + 8, :], 0.0)
+        totals = [
+            t + jnp.where(fault == s + 1.0, value, 0.0) for s, t in enumerate(totals)
+        ]
+    total = jnp.concatenate([merge_rows(totals[i : i + 8]) for i in range(0, faults, 8)], axis=0)
+    total = jnp.sum(total, axis=1, keepdims=True)
+    mine = row_iota((faults, 128)) == lax.broadcasted_iota(I32, (faults, 128), 1)
+    grad = jnp.sum(jnp.where(mine, total, 0.0), axis=0)
+    grad_ref[...] = grad[0:faults] / slip_ref[...]
 
 
 def body(
@@ -714,19 +748,19 @@
         compiler_params=pltpu.CompilerParams(vmem_limit_bytes=2 * MIB),
     )(place, gauge_row, gauge_col, observed)
 
-    slots_view = recv_flat.reshape(devices, 1, CHUNK * 128)
-    eta, west, east, top, bottom = pl.pallas_call(
+    eta, west, east, top, bottom, block_of = pl.pallas_call(
         scatter_kernel,
         out_shape=[f((rows_here, cols_here), F32)]
         + [f((32, rows_here), F32)] * 2
-        + [f((32, cols_here), F32)] * 2,
-        in_specs=[hbm()] + [vmem()] * 6 + [hbm()],
-        out_specs=[vmem()] * 5,
-        scratch_shapes=[pltpu.SMEM((devices, 1, 128), F32), pltpu.SemaphoreType.DMA]
+        + [f((32, cols_here), F32)] * 2
+        + [f((8, devices), I32)],
+        in_specs=[vmem()] * 6 + [hbm()],
+        out_specs=[vmem()] * 6,
+        scratch_shapes=[pltpu.SMEM((8, devices), I32), pltpu.SemaphoreType.DMA]
         + [pltpu.VMEM((rows_here * cols_here // 1024, 8, 128), F32)] * SLOTS,
         name="scatter",
         compiler_params=pltpu.CompilerParams(vmem_limit_bytes=10 * MIB),
-    )(slots_view, recv, wet_mask, *edges, token)
+    )(recv, wet_mask, *edges, token)
     from_east = shifted(west, "gy", -1)
     from_west = shifted(east, "gy", 1)
     tiles = (eta, ocean_depth, wet_mask, manning)
@@ -760,47 +794,32 @@
 
     tile = f((rows_here, cols_here), F32)
 
-    def many(n):
-        return pltpu.VMEM((n, rows, cols), F32)
-
     final, adjoint, back = pl.pallas_call(
         solve_kernel,
         out_shape=[tile, tile, f((devices, 128), F32)],
-        in_specs=[smem()] * 3 + [vmem()] * 38 + [hbm()],
+        in_specs=[smem()] * 3 + [vmem()] * 38 + [smem()],
         out_specs=[vmem()] * 3,
-        scratch_shapes=[
-            many(steps - 1),
-            many(steps - 2),
-            many(steps - 1),
-            many(steps - 2),
-            many(steps - 2),
-            many(steps - 1),
-            many(steps - 1),
-            *[pltpu.VMEM((rows, cols), F32)] * 8,
+        scratch_shapes=[pltpu.VMEM((rows, cols), F32)] * (4 * (steps - 1) + 3 * (steps - 2) + 8)
+        + [
             pltpu.VMEM((rows_here // 8 * (cols_here // 128), 8, 128), F32),
             pltpu.VMEM((SLOTS, devices, 128), F32),
             pltpu.VMEM((steps * per_tile, 128), F32),
-            pltpu.SMEM((devices, 1, 128), F32),
-            pltpu.SemaphoreType.DMA,
         ],
         compiler_params=pltpu.CompilerParams(vmem_limit_bytes=26 * MIB),
         name="solve",
     )(
         place, gauge_row, gauge_col, *made, *framed,
-        from_north, from_south, top, bottom, count, obs, recv, slots_view,
+        from_north, from_south, top, bottom, count, obs, recv, block_of,
     )
     returned = lax.all_to_all(back, both, split_axis=0, concat_axis=0, tiled=True)
-    readings = (
-        returned[:, SLOTS : SLOTS + steps * per_tile]
-        .reshape(devices, steps, per_tile)
-        .transpose(1, 0, 2)
-        .reshape(steps, gauges)
-    )
-    fault_of = table[:, 8 : 8 + SLOTS].astype(I32) - 1
-    mine = fault_of[:, :, None] == jnp.arange(faults, dtype=I32)[None, None, :]
-    grad_slip = (
-        jnp.sum(jnp.where(mine, returned[:, :SLOTS, None], 0.0), axis=(0, 1)) / fault_slip
-    )
+    readings, grad_slip = pl.pallas_call(
+        closing_kernel,
+        out_shape=[f((steps, gauges), F32), f((faults,), F32)],
+        in_specs=[vmem()] * 3,
+        out_specs=[vmem()] * 2,
+        compiler_params=pltpu.CompilerParams(vmem_limit_bytes=MIB),
+        name="closing",
+    )(returned, table, fault_slip)
     return (final, readings, adjoint, grad_slip)
 
 

time: 110 us -> 107 us (0.973)
  blocking collectives: 0 us -> 18.2 us
  waiting for transfers between devices: 33.2 us -> 23.5 us
  starting transfers between devices: 32 us -> 23.5 us
  Pallas kernels: 38.1 us -> 36.6 us
    all_to_all x0 -> x1, blocking collectives: none -> 18.2 us  [body(): lax.all_to_all(back, both, split_axis=0, concat_axis=0, tiled=True)]
    all_to_all x1 -> x0, waiting for transfers between devices: 9.73 us -> none  [body(): lax.all_to_all(back, both, split_axis=0, concat_axis=0, tiled=True)]
    all_to_all x1 -> x0, starting transfers between devices: 8.49 us -> none  [body(): lax.all_to_all(back, both, split_axis=0, concat_axis=0, tiled=True)]
    pallas_call x1, Pallas kernels: 3.23 us -> 1.95 us  [body(): pl.pallas_call(scatter_kernel, out_shape=[f((rows_here, cols_here), F32)]...]
  transfers between devices with their start and end apart: 6 -> 5, of which waited for: 3 -> 2; matrix products, arithmetic and copies ran while one was open for 0% -> 0% of each run, Pallas kernels for 10% -> 10%
where the time goes in v3:
time: 107 us; the launch traced here: 106 us
  Pallas kernels  36.6 us (34%)
  starting transfers between devices  23.5 us (22%)
  waiting for transfers between devices  23.5 us (22%)
  blocking collectives  18.2 us (17%)
  local copies, waits for them, and re-layouts  3.55 us (3%)
    all_to_all x1, waiting for transfers between devices, body(): lax.all_to_all(packed.reshape(-1), both, split_axis=0, concat_axis=0, til...  21.3 us
    pallas_call x1, Pallas kernels, body(): pl.pallas_call(solve_kernel, out_shape=[tile, tile, f((devices, 128), F32...  19.3 us
    all_to_all x1, blocking collectives, body(): lax.all_to_all(back, both, split_axis=0, concat_axis=0, tiled=True)  18.2 us
    ppermute x4, starting transfers between devices, shifted(): return lax.ppermute(shard, axis, pairs)  12 us
    all_to_all x1, starting transfers between devices, body(): lax.all_to_all(packed.reshape(-1), both, split_axis=0, concat_axis=0, til...  11.5 us
    pallas_call x1, Pallas kernels, body(): pl.pallas_call(gauge_kernel, out_shape=[grid, f((steps, rows, cols), F32)...  5.14 us
    pallas_call x1, Pallas kernels, body(): pl.pallas_call(pack_kernel, out_shape=[f((devices * CHUNK, 128), F32), f(...  3.59 us
    unnamed x26, local copies, waits for them, and re-layouts  3.55 us
  transfers between devices with their start and end apart: 5, of which 2 were waited for; matrix products, arithmetic and copies ran while one was open for 0% of the time, Pallas kernels for 10%

profile of v3, /device:TPU:1, one launch (start us, length us, event | category | flops | bytes accessed | tf_op | source)
XLA Modules:
  0.0 106.3 jit_solution(12334294405630295376)
XLA Ops:
  0.6 3.6 %pack.1 = (f32[4224,128]{1,0:T(8,128)}, f32[128,128]{1,0:T(8,128)}) custom-call(f32[16]{0:T(128)} %slip_ref.3, s32[1,256]{1,0:T(1,128)} %bitcast.15, s32[1,256]{1,0:T(1,128)} %bitcast.16, f32[256,8,128]{2,1,0:T(8,128)} %pattern_hbm.1), custom_call_target="tpu_custom_call" | custom-call | tf_op jit(solution)/shard_map/pack/pallas_call | solution.py:713
  4.2 0.0 copy-start
  4.2 0.0 copy-start.1
  4.3 0.0 copy-start.9
  4.3 0.0 copy-start.10
  4.3 0.0 copy-start.11
  4.3 11.5 %all-to-all-start = ((f32[128,4224,1]{1,2,0:T(1,128)}), f32[128,4224,1]{1,2,0:T(1,128)S(1)}, u32[]{:S(2)}, u32[]{:S(2)}) async-start(f32[128,4224,1]{1,2,0:T(1,128)} %bitcast.14), calls=%async_computation | async-start | bytes 4325376 | tf_op jit(solution)/shard_map/all_to_all | solution.py:726
  15.8 0.0 copy-start.2
  15.8 1.0 copy-done.2
  16.9 0.1 static_edges.1
  17.0 0.1 pad_add_fusion.place_ref.refs_0_
  17.1 0.0 copy-done.10
  17.1 0.0 copy-done.11
  17.1 5.1 %gauges.1 = (f32[272,640]{1,0:T(8,128)S(1)}, f32[4,272,640]{2,1,0:T(8,128)S(1)}, f32[8,128]{1,0:T(8,128)S(1)}) custom-call(s32[4]{0:T(128)S(1)} %pad_add_fusion.place_ref.refs_0_, s32[2048]{0:T(1024)S(1)} %copy-done.9, s32[2048]{0:T(1024)S(1)} %copy-done.10, f32[4,2048]{1,0:T(4,128)S(1)} %copy-done.11), custom_call_target="tpu_custom_call" | custom-call | tf_op jit(solution)/shard_map/gauges/pallas_call | solution.py:742
  22.3 1.6 %copy-done.4 = f32[4,272,640]{2,1,0:T(8,128)} copy-done((f32[4,272,640]{2,1,0:T(8,128)}, f32[4,272,640]{2,1,0:T(8,128)S(1)}, u32[]{:S(2)}) %copy-start.4) | copy-done | bytes 2785304
  23.8 0.9 copy-done.6
  24.7 21.3 %all-to-all-done = f32[128,4224,1]{1,2,0:T(1,128)S(1)} async-done(((f32[128,4224,1]{1,2,0:T(1,128)}), f32[128,4224,1]{1,2,0:T(1,128)S(1)}, u32[]{:S(2)}, u32[]{:S(2)}) %all-to-all-start) | async-done | bytes 2162720 | tf_op jit(solution)/shard_map/all_to_all | solution.py:726
  46.0 2.0 %scatter.1 = (f32[256,512]{1,0:T(8,128)S(1)}, f32[32,256]{1,0:T(8,128)S(1)}, f32[32,256]{1,0:T(8,128)S(1)}, f32[32,512]{1,0:T(8,128)S(1)}, f32[32,512]{1,0:T(8,128)S(1)}, /*index=5*/s32[8,128]{1,0:T(8,128)S(1)}) custom-call(f32[4224,128]{1,0:T(8,128)S(1)} %bitcast.10, s32[256,512]{1,0:T(8,128)S(1)} %copy-done, f32[24,256]{1,0:T(8,128)S(1)} %get-tuple-element.58.west_in, ...), custom_call_target="tpu_custom_call" | custom-call | tf_op jit(solution)/shard_map/scatter/pallas_call | solution.py:751
  48.0 1.3 %collective-permute-start = (f32[32,256]{1,0:T(8,128)S(1)}, f32[32,256]{1,0:T(8,128)S(1)}, u32[]{:S(2)}, u32[]{:S(2)}) collective-permute-start(f32[32,256]{1,0:T(8,128)S(1)} %get-tuple-element.76), channel_id=1, source_target_pairs={{1,0},{2,1},{3,2},{4,3},{5,4},{6,5},{7,6},{9,8},{10,9},{11,10},{12... | collective-permute-start | bytes 98312 | tf_op jit(solution)/shard_map/ppermute | solution.py:43
  49.3 4.0 %collective-permute-start.1 = (f32[32,256]{1,0:T(8,128)S(1)}, f32[32,256]{1,0:T(8,128)S(1)}, u32[]{:S(2)}, u32[]{:S(2)}) collective-permute-start(f32[32,256]{1,0:T(8,128)S(1)} %get-tuple-element.77), channel_id=1, source_target_pairs={{0,1},{1,2},{2,3},{3,4},{4,5},{5,6},{6,7},{8,9},{9,10},{10,11},{11... | collective-permute-start | bytes 98312 | tf_op jit(solution)/shard_map/ppermute | solution.py:43
  53.3 2.3 %tile.1 = (f32[272,640]{1,0:T(8,128)S(1)}, f32[272,640]{1,0:T(8,128)S(1)}, f32[272,640]{1,0:T(8,128)S(1)}, f32[272,640]{1,0:T(8,128)S(1)}, f32[272,640]{1,0:T(8,...) custom-call(f32[256,512]{1,0:T(8,128)S(1)} %get-tuple-element.63.eta, ...), custom_call_target="tpu_custom_call" | custom-call | tf_op jit(solution)/shard_map/tile/pallas_call | solution.py:767
  55.6 0.0 collective-permute-done.east_ref
  55.6 0.0 collective-permute-done.1.west_ref
  55.6 0.1 rims.1
  55.8 4.8 %collective-permute-start.2 = (f32[32,640]{1,0:T(8,128)S(1)}, f32[32,640]{1,0:T(8,128)S(1)}, u32[]{:S(2)}, u32[]{:S(2)}) collective-permute-start(f32[32,640]{1,0:T(8,128)S(1)} %get-tuple-element.99.refs_37_), channel_id=1, source_target_pairs={{0,8},{8,16},{16,24},{24,32},{32,40},{40,48},{48,56},{56,64},{64,7... | collective-permute-start | bytes 245768 | tf_op jit(solution)/shard_map/ppermute | solution.py:43
  60.6 1.9 %collective-permute-start.3 = (f32[32,640]{1,0:T(8,128)S(1)}, f32[32,640]{1,0:T(8,128)S(1)}, u32[]{:S(2)}, u32[]{:S(2)}) collective-permute-start(f32[32,640]{1,0:T(8,128)S(1)} %get-tuple-element.100.refs_36_), channel_id=1, source_target_pairs={{8,0},{16,8},{24,16},{32,24},{40,32},{48,40},{56,48},{64,56},{72,6... | collective-permute-start | bytes 245768 | tf_op jit(solution)/shard_map/ppermute | solution.py:43
  62.5 3.1 %frame.1 = (f32[272,256]{1,0:T(8,128)S(1)}, f32[272,256]{1,0:T(8,128)S(1)}, f32[272,256]{1,0:T(8,128)S(1)}, f32[272,256]{1,0:T(8,128)S(1)}, f32[272,256]{1,0:T(8...) custom-call(f32[256,512]{1,0:T(8,128)S(1)} %get-tuple-element.63.eta, ...), custom_call_target="tpu_custom_call" | custom-call | tf_op jit(solution)/shard_map/frame/pallas_call | solution.py:785
  65.7 0.0 collective-permute-done.2.refs_34_
  65.7 2.1 %collective-permute-done.3.refs_35_ = f32[32,640]{1,0:T(8,128)S(1)} collective-permute-done((f32[32,640]{1,0:T(8,128)S(1)}, f32[32,640]{1,0:T(8,128)S(1)}, u32[]{:S(2)}, u32[]{:S(2)}) %collective-permute-start.3) | collective-permute-done | bytes 81952 | tf_op jit(solution)/shard_map/ppermute | solution.py:43
  67.9 19.3 %solve.1 = (f32[256,512]{1,0:T(8,128)}, f32[256,512]{1,0:T(8,128)}, f32[128,128]{1,0:T(8,128)S(1)}) custom-call(s32[4]{0:T(128)S(1)} %pad_add_fusion.place_ref.refs_0_, s32[2048]{0:T(1024)S(1)} %copy-done.9, s32[2048]{0:T(1024)S(1)} %copy-done.10, f32[272,640]{1,0:T(8,128)S(1)} %get-tuple-element.64.dde.after.refs_3_, ...), custom_call_target="tpu_custom_call" | custom-call | tf_op jit(solution)/shard_map/solve/pallas_call | solution.py:797
  87.2 18.2 %all_to_all.20 = f32[128,1,128]{2,1,0:T(1,128)S(1)} all-to-all(f32[128,1,128]{2,1,0:T(1,128)S(1)} %bitcast.13), channel_id=1, replica_groups=mesh['gx'=16,'gy'=8] {'gx','gy'}, dimensions={0} | all-to-all | bytes 131072 | tf_op jit(solution)/shard_map/all_to_all | solution.py:814
  105.4 0.9 closing.1
  (15 shorter events, 0.0 us)
Async XLA Ops:
  4.2 11.6 %copy-start = (s32[256,512]{1,0:T(8,128)S(1)}, s32[256,512]{1,0:T(8,128)}, u32[]{:S(2)}) copy-start(s32[256,512]{1,0:T(8,128)} %wet_ref.7) | copy-start | bytes 1572868
  4.2 11.6 %copy-start.1 = (f32[256,512]{1,0:T(8,128)S(1)}, f32[256,512]{1,0:T(8,128)}, u32[]{:S(2)}) copy-start(f32[256,512]{1,0:T(8,128)} %depth_ref.5) | copy-start | bytes 1572868
  4.3 12.8 %copy-start.9 = (s32[2048]{0:T(1024)S(1)}, s32[2048]{0:T(1024)}, u32[]{:S(2)}) copy-start(s32[2048]{0:T(1024)} %refs_1_.1) | copy-start | bytes 24580
  4.3 12.8 %copy-start.10 = (s32[2048]{0:T(1024)S(1)}, s32[2048]{0:T(1024)}, u32[]{:S(2)}) copy-start(s32[2048]{0:T(1024)} %refs_2_.1) | copy-start | bytes 24580
  4.3 12.8 %copy-start.11 = (f32[4,2048]{1,0:T(4,128)S(1)}, f32[4,2048]{1,0:T(4,128)}, u32[]{:S(2)}) copy-start(f32[4,2048]{1,0:T(4,128)} %obs_ref.1) | copy-start | bytes 98308
  4.3 41.7 %all-to-all-start = ((f32[128,4224,1]{1,2,0:T(1,128)}), f32[128,4224,1]{1,2,0:T(1,128)S(1)}, u32[]{:S(2)}, u32[]{:S(2)}) async-start(f32[128,4224,1]{1,2,0:T(1,128)} %bitcast.14), calls=%async_computation | async-start | bytes 4325376 | tf_op jit(solution)/shard_map/all_to_all | solution.py:726
  15.8 1.0 copy-start.2
  22.3 1.6 %copy-start.4 = (f32[4,272,640]{2,1,0:T(8,128)}, f32[4,272,640]{2,1,0:T(8,128)S(1)}, u32[]{:S(2)}) copy-start(f32[4,272,640]{2,1,0:T(8,128)S(1)} %get-tuple-element.102.refs_39_) | copy-start | bytes 8355844
  23.8 0.9 copy-start.6
  46.0 7.3 %copy-start.3 = (f32[256,512]{1,0:T(8,128)S(1)}, f32[256,512]{1,0:T(8,128)}, u32[]{:S(2)}) copy-start(f32[256,512]{1,0:T(8,128)} %fric_ref.5) | copy-start | bytes 1572868
  48.0 7.6 %collective-permute-start = (f32[32,256]{1,0:T(8,128)S(1)}, f32[32,256]{1,0:T(8,128)S(1)}, u32[]{:S(2)}, u32[]{:S(2)}) collective-permute-start(f32[32,256]{1,0:T(8,128)S(1)} %get-tuple-element.76), channel_id=1, source_target_pairs={{1,0},{2,1},{3,2},{4,3},{5,4},{6,5},{7,6},{9,8},{10,9},{11,10},{12... | collective-permute-start | bytes 98312 | tf_op jit(solution)/shard_map/ppermute | solution.py:43
  49.3 6.3 %collective-permute-start.1 = (f32[32,256]{1,0:T(8,128)S(1)}, f32[32,256]{1,0:T(8,128)S(1)}, u32[]{:S(2)}, u32[]{:S(2)}) collective-permute-start(f32[32,256]{1,0:T(8,128)S(1)} %get-tuple-element.77), channel_id=1, source_target_pairs={{0,1},{1,2},{2,3},{3,4},{4,5},{5,6},{6,7},{8,9},{9,10},{10,11},{11... | collective-permute-start | bytes 98312 | tf_op jit(solution)/shard_map/ppermute | solution.py:43
  55.8 9.9 %collective-permute-start.2 = (f32[32,640]{1,0:T(8,128)S(1)}, f32[32,640]{1,0:T(8,128)S(1)}, u32[]{:S(2)}, u32[]{:S(2)}) collective-permute-start(f32[32,640]{1,0:T(8,128)S(1)} %get-tuple-element.99.refs_37_), channel_id=1, source_target_pairs={{0,8},{8,16},{16,24},{24,32},{32,40},{40,48},{48,56},{56,64},{64,7... | collective-permute-start | bytes 245768 | tf_op jit(solution)/shard_map/ppermute | solution.py:43
  60.6 7.3 %collective-permute-start.3 = (f32[32,640]{1,0:T(8,128)S(1)}, f32[32,640]{1,0:T(8,128)S(1)}, u32[]{:S(2)}, u32[]{:S(2)}) collective-permute-start(f32[32,640]{1,0:T(8,128)S(1)} %get-tuple-element.100.refs_36_), channel_id=1, source_target_pairs={{8,0},{16,8},{24,16},{32,24},{40,32},{48,40},{56,48},{64,56},{72,6... | collective-permute-start | bytes 245768 | tf_op jit(solution)/shard_map/ppermute | solution.py:43
  62.5 5.3 %copy-start.5 = (f32[4,272,640]{2,1,0:T(8,128)S(1)}, f32[4,272,640]{2,1,0:T(8,128)}, u32[]{:S(2)}) copy-start(f32[4,272,640]{2,1,0:T(8,128)} %copy-done.4) | copy-start | bytes 8355844
  62.5 5.3 %copy-start.7 = (f32[272,640]{1,0:T(8,128)S(1)}, f32[272,640]{1,0:T(8,128)}, u32[]{:S(2)}) copy-start(f32[272,640]{1,0:T(8,128)} %copy-done.6) | copy-start | bytes 2088964
  67.9 37.5 %copy-start.8 = (f32[128,128]{1,0:T(8,128)S(1)}, f32[128,128]{1,0:T(8,128)}, u32[]{:S(2)}) copy-start(f32[128,128]{1,0:T(8,128)} %get-tuple-element.106.table_ref) | copy-start | bytes 196612
  67.9 37.5 %copy-start.12 = (f32[16]{0:T(128)S(1)}, f32[16]{0:T(128)}, u32[]{:S(2)}) copy-start(f32[16]{0:T(128)} %slip_ref.3) | copy-start | bytes 196

commit v4 on v3

--- a/solution.py
+++ b/solution.py
@@ -37,10 +37,14 @@
     return pl.BlockSpec(memory_space=pl.ANY)
 
 
-def shifted(shard, axis, by):
+def swapped(shard, axis, first):
     devices = lax.axis_size(axis)
-    pairs = [(i, i + by) for i in range(devices) if 0 <= i + by < devices]
-    return lax.ppermute(shard, axis, pairs)
+    pairs = [(i, i + 1) for i in range(first, devices - 1, 2)]
+    return lax.ppermute(shard, axis, pairs + [(j, i) for i, j in pairs])
+
+
+def by_parity(index, even, odd):
+    return jnp.where(index % 2 == 0, even, odd)
 
 
 def pack_kernel(
@@ -111,10 +115,11 @@
 
 
 def scatter_kernel(
-    recv_ref, wet_ref, west_in, east_in, top_in, bottom_in, after,
-    eta_ref, west_ref, east_ref, top_ref, bottom_ref, block_out, block_s, sem, *acc,
+    place_ref, recv_ref, wet_ref, west_in, east_in, top_in, bottom_in, after,
+    eta_ref, one_ref, two_ref, top_ref, bottom_ref, block_out, block_s, sem, *acc,
 ):
     del after
+    gy = place_ref[1]
     tiles = recv_ref.shape[0] // CHUNK
     facts = recv_ref[pl.ds(8 * SLOTS, tiles, stride=CHUNK), :]
     block_out[...] = facts.T[0:8].astype(I32)
@@ -130,10 +135,10 @@
         return c
 
     lax.fori_loop(0, acc[0].shape[0], clear, 0, unroll=8)
-    for dst, src in (
-        (west_ref, west_in), (east_ref, east_in), (top_ref, top_in), (bottom_ref, bottom_in)
-    ):
-        dst[0:24, :] = src[...]
+    one_ref[0:24, :] = by_parity(gy, east_in[...], west_in[...])
+    two_ref[0:24, :] = by_parity(gy, west_in[...], east_in[...])
+    top_ref[0:24, :] = top_in[...]
+    bottom_ref[0:24, :] = bottom_in[...]
     load.wait()
 
     def add(i, c):
@@ -157,8 +162,8 @@
 
     lax.fori_loop(0, rows // 8, merge, 0, unroll=2)
     west, east = edges_of(eta_ref[:, 0:128], eta_ref[:, cols - 128 : cols])
-    west_ref[24:32] = west
-    east_ref[24:32] = east
+    one_ref[24:32] = by_parity(gy, east, west)
+    two_ref[24:32] = by_parity(gy, west, east)
     top_ref[24:32] = eta_ref[0:8, :]
     bottom_ref[24:32] = eta_ref[rows - 8 : rows, :]
 
@@ -176,11 +181,16 @@
         bottom_ref[at] = ref[rows - 8 : rows, :].astype(F32)
 
 
-def rim_kernel(east_ref, west_ref, top_in, bottom_in, after, top_ref, bottom_ref):
+def rim_kernel(
+    place_ref, one_in, two_in, top_in, bottom_in, after, top_ref, bottom_ref, one_ref, two_ref
+):
     del after
-    fields = east_ref.shape[0] // 8
-    rows = east_ref.shape[1]
+    fields = one_in.shape[0] // 8
+    rows = one_in.shape[1]
     cols = top_in.shape[1]
+    gx, gy = place_ref[0], place_ref[1]
+    east_ref = by_parity(gy, one_in[...], two_in[...])
+    west_ref = by_parity(gy, two_in[...], one_in[...])
     lane = lax.broadcasted_iota(I32, (8, 128), 1)
     for src, out, first, keep in (
         (top_in, top_ref, 0, slice(0, 8)),
@@ -198,6 +208,8 @@
             out[at, cols:] = jnp.where(
                 (lane < 8) | (lane >= 120), pltpu.roll(corners, 128 - 16 * n - 8, 1), 0.0
             )
+    one_ref[...] = by_parity(gx, bottom_ref[...], top_ref[...])
+    two_ref[...] = by_parity(gx, top_ref[...], bottom_ref[...])
 
 
 def row_iota(shape):
@@ -340,7 +352,7 @@
 
 
 def frame_kernel(
-    eta_ref, depth_ref, wet_ref, fric_ref, east_ref, west_ref, dde, rre, wwe, fe, fs, *refs
+    place_ref, eta_ref, depth_ref, wet_ref, fric_ref, one_in, two_in, dde, rre, wwe, fe, fs, *refs
 ):
     east, south = refs[:6], refs[6:12]
     surf0, wet, surf1, fe1, ae1, pe1, qe1 = refs[12:19]
@@ -348,8 +360,10 @@
     rows, cols = eta_ref.shape
     fields = (depth_ref, wet_ref, fric_ref, eta_ref)
     blocks = rows // 8
+    gy = place_ref[1]
     for n, side in enumerate(sides):
-        side[...] = side_block(east_ref[8 * n : 8 * n + 8], west_ref[8 * n : 8 * n + 8])
+        one, two = one_in[8 * n : 8 * n + 8], two_in[8 * n : 8 * n + 8]
+        side[...] = side_block(by_parity(gy, one, two), by_parity(gy, two, one))
 
     def frame(i, c):
         at = rows_at(i)
@@ -405,7 +419,7 @@
     place_ref, grow_ref, gcol_ref = refs[:3]
     east0, south0, east_part, south_part = (refs[3 + 6 * n : 9 + 6 * n] for n in range(4))
     surf0, wet, surf1, fe1, ae1, pe1, qe1 = refs[27:34]
-    north_ref, south_ref, top_ref, bottom_ref, count, obs, recv, block_ref = refs[34:42]
+    one_in, two_in, top_ref, bottom_ref, count, obs, recv, block_ref = refs[34:42]
     final_ref, adj_ref, back_ref = refs[42:45]
     steps, rows, cols = obs.shape
     scratch = list(refs[45:])
@@ -425,7 +439,9 @@
     qe = [qe0, qe1] + take_scratch(steps - 2)
     ps = [ps0] + take_scratch(steps - 1)
     qs = [qs0] + take_scratch(steps - 1)
-    adj, ce, cs, spread, turned, west, xe, xs, grads, parts, reads = scratch
+    adj, ce, cs, spread, turned, west, xe, xs, grads, parts, reads, north_ref, south_ref = scratch
+    south_ref[...] = by_parity(place_ref[0], one_in[...], two_in[...])
+    north_ref[...] = by_parity(place_ref[0], two_in[...], one_in[...])
     sub = row_iota((8, cols))
     last = sub == 7
     firstrow = sub == 0
@@ -748,21 +764,20 @@
         compiler_params=pltpu.CompilerParams(vmem_limit_bytes=2 * MIB),
     )(place, gauge_row, gauge_col, observed)
 
-    eta, west, east, top, bottom, block_of = pl.pallas_call(
+    eta, one, two, top, bottom, block_of = pl.pallas_call(
         scatter_kernel,
         out_shape=[f((rows_here, cols_here), F32)]
         + [f((32, rows_here), F32)] * 2
         + [f((32, cols_here), F32)] * 2
         + [f((8, devices), I32)],
-        in_specs=[vmem()] * 6 + [hbm()],
+        in_specs=[smem()] + [vmem()] * 6 + [hbm()],
         out_specs=[vmem()] * 6,
         scratch_shapes=[pltpu.SMEM((8, devices), I32), pltpu.SemaphoreType.DMA]
         + [pltpu.VMEM((rows_here * cols_here // 1024, 8, 128), F32)] * SLOTS,
         name="scatter",
         compiler_params=pltpu.CompilerParams(vmem_limit_bytes=10 * MIB),
-    )(recv, wet_mask, *edges, token)
-    from_east = shifted(west, "gy", -1)
-    from_west = shifted(east, "gy", 1)
+    )(place, recv, wet_mask, *edges, token)
+    sides = swapped(one, "gy", 0), swapped(two, "gy", 1)
     tiles = (eta, ocean_depth, wet_mask, manning)
     made = pl.pallas_call(
         tile_kernel,
@@ -772,25 +787,24 @@
         compiler_params=pltpu.CompilerParams(vmem_limit_bytes=MIB),
         name="tile",
     )(*tiles)
-    top, bottom = pl.pallas_call(
+    top, bottom, one, two = pl.pallas_call(
         rim_kernel,
-        out_shape=[f((32, cols), F32)] * 2,
-        in_specs=[vmem()] * 4 + [hbm()],
-        out_specs=[vmem()] * 2,
+        out_shape=[f((32, cols), F32)] * 4,
+        in_specs=[smem()] + [vmem()] * 4 + [hbm()],
+        out_specs=[vmem()] * 4,
         compiler_params=pltpu.CompilerParams(vmem_limit_bytes=MIB),
         name="rims",
-    )(from_east, from_west, top, bottom, made[0])
-    from_south = shifted(top, "gx", -1)
-    from_north = shifted(bottom, "gx", 1)
+    )(place, *sides, top, bottom, made[0])
+    ends = swapped(one, "gx", 0), swapped(two, "gx", 1)
     framed = pl.pallas_call(
         frame_kernel,
         out_shape=[f((rows, 256), F32)] * 6 + [f((rows, 128), F32)] * 6 + [grid] * 7,
-        in_specs=[vmem()] * 11,
+        in_specs=[smem()] + [vmem()] * 11,
         out_specs=[vmem()] * 19,
         scratch_shapes=[pltpu.VMEM((rows_here, 128), F32)] * 4,
         compiler_params=pltpu.CompilerParams(vmem_limit_bytes=2 * MIB),
         name="frame",
-    )(*tiles, from_east, from_west, *made[:4], made[9])
+    )(place, *tiles, *sides, *made[:4], made[9])
 
     tile = f((rows_here, cols_here), F32)
 
@@ -804,12 +818,13 @@
             pltpu.VMEM((rows_here // 8 * (cols_here // 128), 8, 128), F32),
             pltpu.VMEM((SLOTS, devices, 128), F32),
             pltpu.VMEM((steps * per_tile, 128), F32),
-        ],
+        ]
+        + [pltpu.VMEM((32, cols), F32)] * 2,
         compiler_params=pltpu.CompilerParams(vmem_limit_bytes=26 * MIB),
         name="solve",
     )(
         place, gauge_row, gauge_col, *made, *framed,
-        from_north, from_south, top, bottom, count, obs, recv, block_of,
+        *ends, top, bottom, count, obs, recv, block_of,
     )
     returned = lax.all_to_all(back, both, split_axis=0, concat_axis=0, tiled=True)
     readings, grad_slip = pl.pallas_call(

time: 107 us -> 101 us (0.944)
  starting transfers between devices: 23.5 us -> 17.5 us
  Pallas kernels: 36.6 us -> 38.4 us
    ppermute x4, starting transfers between devices: 12 us -> 6.05 us  [swapped(): return lax.ppermute(shard, axis, pairs + [(j, i) for i, j in pairs])]
  transfers between devices with their start and end apart: 5 -> 5, of which waited for: 2 -> 2; matrix products, arithmetic and copies ran while one was open for 0% -> 0% of each run, Pallas kernels for 10% -> 11%
where the time goes in v4:
time: 101 us
  Pallas kernels  38.4 us (38%)
  waiting for transfers between devices  22.6 us (22%)
  blocking collectives  17.7 us (18%)
  starting transfers between devices  17.5 us (17%)
  local copies, waits for them, and re-layouts  3.55 us (4%)
    all_to_all x1, waiting for transfers between devices, body(): lax.all_to_all(packed.reshape(-1), both, split_axis=0, concat_axis=0, til...  21.3 us
    pallas_call x1, Pallas kernels, body(): pl.pallas_call(solve_kernel, out_shape=[tile, tile, f((devices, 128), F32...  19.4 us
    all_to_all x1, blocking collectives, body(): lax.all_to_all(back, both, split_axis=0, concat_axis=0, tiled=True)  17.7 us
    all_to_all x1, starting transfers between devices, body(): lax.all_to_all(packed.reshape(-1), both, split_axis=0, concat_axis=0, til...  11.5 us
    ppermute x4, starting transfers between devices, swapped(): return lax.ppermute(shard, axis, pairs + [(j, i) for i, j in pairs])  6.05 us
    pallas_call x1, Pallas kernels, body(): pl.pallas_call(gauge_kernel, out_shape=[grid, f((steps, rows, cols), F32)...  5.16 us
    pallas_call x1, Pallas kernels, body(): pl.pallas_call(frame_kernel, out_shape=[f((rows, 256), F32)] * 6 + [f((ro...  3.71 us
    pallas_call x1, Pallas kernels, body(): pl.pallas_call(pack_kernel, out_shape=[f((devices * CHUNK, 128), F32), f(...  3.59 us
  transfers between devices with their start and end apart: 5, of which 2 were waited for; matrix products, arithmetic and copies ran while one was open for 0% of the time, Pallas kernels for 11%

profile of v4, /device:TPU:1, one launch (start us, length us, event | category | flops | bytes accessed | tf_op | source)
XLA Modules:
  0.0 100.8 jit_solution(9266129342572016123)
XLA Ops:
  0.6 3.6 %pack.1 = (f32[4224,128]{1,0:T(8,128)}, f32[128,128]{1,0:T(8,128)}) custom-call(f32[16]{0:T(128)} %slip_ref.3, s32[1,256]{1,0:T(1,128)} %bitcast.15, s32[1,256]{1,0:T(1,128)} %bitcast.16, f32[256,8,128]{2,1,0:T(8,128)} %pattern_hbm.1), custom_call_target="tpu_custom_call" | custom-call | tf_op jit(solution)/shard_map/pack/pallas_call | solution.py:729
  4.2 0.0 copy-start
  4.2 0.0 copy-start.1
  4.3 0.0 copy-start.9
  4.3 0.0 copy-start.10
  4.3 0.0 copy-start.11
  4.3 11.5 %all-to-all-start = ((f32[128,4224,1]{1,2,0:T(1,128)}), f32[128,4224,1]{1,2,0:T(1,128)S(1)}, u32[]{:S(2)}, u32[]{:S(2)}) async-start(f32[128,4224,1]{1,2,0:T(1,128)} %bitcast.14), calls=%async_computation | async-start | bytes 4325376 | tf_op jit(solution)/shard_map/all_to_all | solution.py:742
  15.8 0.0 copy-start.2
  15.8 1.0 %copy-done.2 = f32[256,512]{1,0:T(8,128)S(1)} copy-done((f32[256,512]{1,0:T(8,128)S(1)}, f32[256,512]{1,0:T(8,128)}, u32[]{:S(2)}) %copy-start.2) | copy-done | bytes 524312
  16.9 0.1 static_edges.1
  17.0 0.1 pad_add_fusion.place_ref.refs_0_
  17.1 0.0 copy-done.10
  17.1 0.0 copy-done.11
  17.1 5.2 %gauges.1 = (f32[272,640]{1,0:T(8,128)S(1)}, f32[4,272,640]{2,1,0:T(8,128)S(1)}, f32[8,128]{1,0:T(8,128)S(1)}) custom-call(s32[4]{0:T(128)S(1)} %pad_add_fusion.place_ref.refs_0_, s32[2048]{0:T(1024)S(1)} %copy-done.9, s32[2048]{0:T(1024)S(1)} %copy-done.10, f32[4,2048]{1,0:T(4,128)S(1)} %copy-done.11), custom_call_target="tpu_custom_call" | custom-call | tf_op jit(solution)/shard_map/gauges/pallas_call | solution.py:758
  22.3 1.6 %copy-done.4 = f32[4,272,640]{2,1,0:T(8,128)} copy-done((f32[4,272,640]{2,1,0:T(8,128)}, f32[4,272,640]{2,1,0:T(8,128)S(1)}, u32[]{:S(2)}) %copy-start.4) | copy-done | bytes 2785304
  23.9 0.9 copy-done.6
  24.7 21.3 %all-to-all-done = f32[128,4224,1]{1,2,0:T(1,128)S(1)} async-done(((f32[128,4224,1]{1,2,0:T(1,128)}), f32[128,4224,1]{1,2,0:T(1,128)S(1)}, u32[]{:S(2)}, u32[]{:S(2)}) %all-to-all-start) | async-done | bytes 2162720 | tf_op jit(solution)/shard_map/all_to_all | solution.py:742
  46.0 2.5 %scatter.1 = (f32[256,512]{1,0:T(8,128)S(1)}, f32[32,256]{1,0:T(8,128)S(1)}, f32[32,256]{1,0:T(8,128)S(1)}, f32[32,512]{1,0:T(8,128)S(1)}, f32[32,512]{1,0:T(8,128)S(1)}, /*index=5*/s32[8,128]{1,0:T(8,128)S(1)}) custom-call(s32[4]{0:T(128)S(1)} %pad_add_fusion.place_ref.refs_0_, f32[4224,128]{1,0:T(8,128)S(1)} %bitcast.10, s32[256,512]{1,0:T(8,128)S(1)} %copy-done, ...), custom_call_target="tpu_custom_call" | custom-call | tf_op jit(solution)/shard_map/scatter/pallas_call | solution.py:767
  48.5 0.5 collective-permute-start
  49.1 0.7 collective-permute-start.1
  49.7 2.3 %tile.1 = (f32[272,640]{1,0:T(8,128)S(1)}, f32[272,640]{1,0:T(8,128)S(1)}, f32[272,640]{1,0:T(8,128)S(1)}, f32[272,640]{1,0:T(8,128)S(1)}, f32[272,640]{1,0:T(8,...) custom-call(f32[256,512]{1,0:T(8,128)S(1)} %get-tuple-element.65.eta, ...), custom_call_target="tpu_custom_call" | custom-call | tf_op jit(solution)/shard_map/tile/pallas_call | solution.py:782
  52.0 0.0 collective-permute-done.one_in
  52.0 0.0 collective-permute-done.1.two_in
  52.0 0.7 rims.1
  52.7 2.4 %collective-permute-start.2 = (f32[32,640]{1,0:T(8,128)S(1)}, f32[32,640]{1,0:T(8,128)S(1)}, u32[]{:S(2)}, u32[]{:S(2)}) collective-permute-start(f32[32,640]{1,0:T(8,128)S(1)} %get-tuple-element.101), channel_id=1, source_target_pairs={{0,8},{16,24},{32,40},{48,56},{64,72},{80,88},{96,104},{112,120},{... | collective-permute-start | bytes 245768 | tf_op jit(solution)/shard_map/ppermute | solution.py:43
  55.2 2.4 %collective-permute-start.3 = (f32[32,640]{1,0:T(8,128)S(1)}, f32[32,640]{1,0:T(8,128)S(1)}, u32[]{:S(2)}, u32[]{:S(2)}) collective-permute-start(f32[32,640]{1,0:T(8,128)S(1)} %get-tuple-element.102), channel_id=1, source_target_pairs={{8,16},{24,32},{40,48},{56,64},{72,80},{88,96},{104,112},{16,8},{3... | collective-permute-start | bytes 245768 | tf_op jit(solution)/shard_map/ppermute | solution.py:43
  57.6 3.7 %frame.1 = (f32[272,256]{1,0:T(8,128)S(1)}, f32[272,256]{1,0:T(8,128)S(1)}, f32[272,256]{1,0:T(8,128)S(1)}, f32[272,256]{1,0:T(8,128)S(1)}, f32[272,256]{1,0:T(8...) custom-call(s32[4]{0:T(128)S(1)} %pad_add_fusion.place_ref.refs_0_, ...), custom_call_target="tpu_custom_call" | custom-call | tf_op jit(solution)/shard_map/frame/pallas_call | solution.py:799
  61.3 0.0 collective-permute-done.2.refs_34_
  61.4 1.4 %collective-permute-done.3.refs_35_ = f32[32,640]{1,0:T(8,128)S(1)} collective-permute-done((f32[32,640]{1,0:T(8,128)S(1)}, f32[32,640]{1,0:T(8,128)S(1)}, u32[]{:S(2)}, u32[]{:S(2)}) %collective-permute-start.3) | collective-permute-done | bytes 81952 | tf_op jit(solution)/shard_map/ppermute | solution.py:43
  62.7 19.4 %solve.1 = (f32[256,512]{1,0:T(8,128)}, f32[256,512]{1,0:T(8,128)}, f32[128,128]{1,0:T(8,128)S(1)}) custom-call(s32[4]{0:T(128)S(1)} %pad_add_fusion.place_ref.refs_0_, s32[2048]{0:T(1024)S(1)} %copy-done.9, s32[2048]{0:T(1024)S(1)} %copy-done.10, f32[272,640]{1,0:T(8,128)S(1)} %get-tuple-element.66.dde.after.refs_3_, ...), custom_call_target="tpu_custom_call" | custom-call | tf_op jit(solution)/shard_map/solve/pallas_call | solution.py:811
  82.2 17.7 %all_to_all.20 = f32[128,1,128]{2,1,0:T(1,128)S(1)} all-to-all(f32[128,1,128]{2,1,0:T(1,128)S(1)} %bitcast.13), channel_id=1, replica_groups=mesh['gx'=16,'gy'=8] {'gx','gy'}, dimensions={0} | all-to-all | bytes 131072 | tf_op jit(solution)/shard_map/all_to_all | solution.py:829
  99.9 0.9 closing.1
  (15 shorter events, 0.0 us)
Async XLA Ops:
  4.2 11.6 %copy-start = (s32[256,512]{1,0:T(8,128)S(1)}, s32[256,512]{1,0:T(8,128)}, u32[]{:S(2)}) copy-start(s32[256,512]{1,0:T(8,128)} %wet_ref.7) | copy-start | bytes 1572868
  4.2 11.6 %copy-start.1 = (f32[256,512]{1,0:T(8,128)S(1)}, f32[256,512]{1,0:T(8,128)}, u32[]{:S(2)}) copy-start(f32[256,512]{1,0:T(8,128)} %depth_ref.5) | copy-start | bytes 1572868
  4.3 12.8 %copy-start.9 = (s32[2048]{0:T(1024)S(1)}, s32[2048]{0:T(1024)}, u32[]{:S(2)}) copy-start(s32[2048]{0:T(1024)} %refs_1_.1) | copy-start | bytes 24580
  4.3 12.8 %copy-start.10 = (s32[2048]{0:T(1024)S(1)}, s32[2048]{0:T(1024)}, u32[]{:S(2)}) copy-start(s32[2048]{0:T(1024)} %refs_2_.1) | copy-start | bytes 24580
  4.3 12.8 %copy-start.11 = (f32[4,2048]{1,0:T(4,128)S(1)}, f32[4,2048]{1,0:T(4,128)}, u32[]{:S(2)}) copy-start(f32[4,2048]{1,0:T(4,128)} %obs_ref.1) | copy-start | bytes 98308
  4.3 41.7 %all-to-all-start = ((f32[128,4224,1]{1,2,0:T(1,128)}), f32[128,4224,1]{1,2,0:T(1,128)S(1)}, u32[]{:S(2)}, u32[]{:S(2)}) async-start(f32[128,4224,1]{1,2,0:T(1,128)} %bitcast.14), calls=%async_computation | async-start | bytes 4325376 | tf_op jit(solution)/shard_map/all_to_all | solution.py:742
  15.8 1.0 %copy-start.2 = (f32[256,512]{1,0:T(8,128)S(1)}, f32[256,512]{1,0:T(8,128)}, u32[]{:S(2)}) copy-start(f32[256,512]{1,0:T(8,128)} %fric_ref.5) | copy-start | bytes 1572868
  22.3 1.6 %copy-start.4 = (f32[4,272,640]{2,1,0:T(8,128)}, f32[4,272,640]{2,1,0:T(8,128)S(1)}, u32[]{:S(2)}) copy-start(f32[4,272,640]{2,1,0:T(8,128)S(1)} %get-tuple-element.106.refs_39_) | copy-start | bytes 8355844
  23.9 0.9 copy-start.6
  46.0 3.7 %copy-start.3 = (f32[256,512]{1,0:T(8,128)S(1)}, f32[256,512]{1,0:T(8,128)}, u32[]{:S(2)}) copy-start(f32[256,512]{1,0:T(8,128)} %fric_ref.5) | copy-start | bytes 1572868
  48.5 3.5 %collective-permute-start = (f32[32,256]{1,0:T(8,128)S(1)}, f32[32,256]{1,0:T(8,128)S(1)}, u32[]{:S(2)}, u32[]{:S(2)}) collective-permute-start(f32[32,256]{1,0:T(8,128)S(1)} %get-tuple-element.78), channel_id=1, source_target_pairs={{0,1},{2,3},{4,5},{6,7},{1,0},{3,2},{5,4},{7,6},{8,9},{10,11},{12,... | collective-permute-start | bytes 98312 | tf_op jit(solution)/shard_map/ppermute | solution.py:43
  49.1 3.0 %collective-permute-start.1 = (f32[32,256]{1,0:T(8,128)S(1)}, f32[32,256]{1,0:T(8,128)S(1)}, u32[]{:S(2)}, u32[]{:S(2)}) collective-permute-start(f32[32,256]{1,0:T(8,128)S(1)} %get-tuple-element.79), channel_id=1, source_target_pairs={{1,2},{3,4},{5,6},{2,1},{4,3},{6,5},{9,10},{11,12},{13,14},{10,9},... | collective-permute-start | bytes 98312 | tf_op jit(solution)/shard_map/ppermute | solution.py:43
  52.7 8.6 %collective-permute-start.2 = (f32[32,640]{1,0:T(8,128)S(1)}, f32[32,640]{1,0:T(8,128)S(1)}, u32[]{:S(2)}, u32[]{:S(2)}) collective-permute-start(f32[32,640]{1,0:T(8,128)S(1)} %get-tuple-element.101), channel_id=1, source_target_pairs={{0,8},{16,24},{32,40},{48,56},{64,72},{80,88},{96,104},{112,120},{... | collective-permute-start | bytes 245768 | tf_op jit(solution)/shard_map/ppermute | solution.py:43
  55.2 7.5 %collective-permute-start.3 = (f32[32,640]{1,0:T(8,128)S(1)}, f32[32,640]{1,0:T(8,128)S(1)}, u32[]{:S(2)}, u32[]{:S(2)}) collective-permute-start(f32[32,640]{1,0:T(8,128)S(1)} %get-tuple-element.102), channel_id=1, source_target_pairs={{8,16},{24,32},{40,48},{56,64},{72,80},{88,96},{104,112},{16,8},{3... | collective-permute-start | bytes 245768 | tf_op jit(solution)/shard_map/ppermute | solution.py:43
  57.6 5.1 %copy-start.5 = (f32[4,272,640]{2,1,0:T(8,128)S(1)}, f32[4,272,640]{2,1,0:T(8,128)}, u32[]{:S(2)}) copy-start(f32[4,272,640]{2,1,0:T(8,128)} %copy-done.4) | copy-start | bytes 8355844
  57.6 5.1 %copy-start.7 = (f32[272,640]{1,0:T(8,128)S(1)}, f32[272,640]{1,0:T(8,128)}, u32[]{:S(2)}) copy-start(f32[272,640]{1,0:T(8,128)} %copy-done.6) | copy-start | bytes 2088964
  62.7 37.2 %copy-start.8 = (f32[128,128]{1,0:T(8,128)S(1)}, f32[128,128]{1,0:T(8,128)}, u32[]{:S(2)}) copy-start(f32[128,128]{1,0:T(8,128)} %get-tuple-element.110.table_ref) | copy-start | bytes 196612
  62.7 37.2 %copy-start.12 = (f32[16]{0:T(128)S(1)}, f32[16]{0:T(128)}, u32[]{:S(2)}) copy-start(f32[16]{0:T(128)} %slip_ref.3) | copy-start | bytes 196

commit v5 on v4

--- a/solution.py
+++ b/solution.py
@@ -43,8 +43,12 @@
     return lax.ppermute(shard, axis, pairs + [(j, i) for i, j in pairs])
 
 
-def by_parity(index, even, odd):
-    return jnp.where(index % 2 == 0, even, odd)
+def choose(flags, axis, even, odd):
+    flag = flags[8 * axis : 8 * axis + 8, :]
+    rows, cols = even.shape
+    flag = jnp.concatenate([flag] * (cols // 128), axis=1)
+    flag = jnp.concatenate([flag] * (rows // 8), axis=0)
+    return jnp.where(flag > 0.5, even, odd)
 
 
 def pack_kernel(
@@ -115,11 +119,10 @@
 
 
 def scatter_kernel(
-    place_ref, recv_ref, wet_ref, west_in, east_in, top_in, bottom_in, after,
+    flags_ref, recv_ref, wet_ref, west_in, east_in, top_in, bottom_in,
     eta_ref, one_ref, two_ref, top_ref, bottom_ref, block_out, block_s, sem, *acc,
 ):
-    del after
-    gy = place_ref[1]
+    flags = flags_ref[...]
     tiles = recv_ref.shape[0] // CHUNK
     facts = recv_ref[pl.ds(8 * SLOTS, tiles, stride=CHUNK), :]
     block_out[...] = facts.T[0:8].astype(I32)
@@ -135,8 +138,8 @@
         return c
 
     lax.fori_loop(0, acc[0].shape[0], clear, 0, unroll=8)
-    one_ref[0:24, :] = by_parity(gy, east_in[...], west_in[...])
-    two_ref[0:24, :] = by_parity(gy, west_in[...], east_in[...])
+    one_ref[0:24, :] = choose(flags, 1, east_in[...], west_in[...])
+    two_ref[0:24, :] = choose(flags, 1, west_in[...], east_in[...])
     top_ref[0:24, :] = top_in[...]
     bottom_ref[0:24, :] = bottom_in[...]
     load.wait()
@@ -162,8 +165,8 @@
 
     lax.fori_loop(0, rows // 8, merge, 0, unroll=2)
     west, east = edges_of(eta_ref[:, 0:128], eta_ref[:, cols - 128 : cols])
-    one_ref[24:32] = by_parity(gy, east, west)
-    two_ref[24:32] = by_parity(gy, west, east)
+    one_ref[24:32] = choose(flags, 1, east, west)
+    two_ref[24:32] = choose(flags, 1, west, east)
     top_ref[24:32] = eta_ref[0:8, :]
     bottom_ref[24:32] = eta_ref[rows - 8 : rows, :]
 
@@ -182,15 +185,15 @@
 
 
 def rim_kernel(
-    place_ref, one_in, two_in, top_in, bottom_in, after, top_ref, bottom_ref, one_ref, two_ref
+    flags_ref, one_in, two_in, top_in, bottom_in, after, top_ref, bottom_ref, one_ref, two_ref
 ):
     del after
     fields = one_in.shape[0] // 8
     rows = one_in.shape[1]
     cols = top_in.shape[1]
-    gx, gy = place_ref[0], place_ref[1]
-    east_ref = by_parity(gy, one_in[...], two_in[...])
-    west_ref = by_parity(gy, two_in[...], one_in[...])
+    flags = flags_ref[...]
+    east_ref = choose(flags, 1, one_in[...], two_in[...])
+    west_ref = choose(flags, 1, two_in[...], one_in[...])
     lane = lax.broadcasted_iota(I32, (8, 128), 1)
     for src, out, first, keep in (
         (top_in, top_ref, 0, slice(0, 8)),
@@ -208,16 +211,18 @@
             out[at, cols:] = jnp.where(
                 (lane < 8) | (lane >= 120), pltpu.roll(corners, 128 - 16 * n - 8, 1), 0.0
             )
-    one_ref[...] = by_parity(gx, bottom_ref[...], top_ref[...])
-    two_ref[...] = by_parity(gx, top_ref[...], bottom_ref[...])
+    one_ref[...] = choose(flags, 0, bottom_ref[...], top_ref[...])
+    two_ref[...] = choose(flags, 0, top_ref[...], bottom_ref[...])
 
 
 def row_iota(shape):
     return lax.broadcasted_iota(I32, shape, 0)
 
 
-def gauge_kernel(place_ref, row_ref, col_ref, obs_ref, count_out, obs_out, token_out):
-    token_out[...] = jnp.zeros(token_out.shape, F32)
+def gauge_kernel(place_ref, row_ref, col_ref, obs_ref, count_out, obs_out, flags_out):
+    for n in range(2):
+        even = jnp.where(place_ref[n] % 2 == 0, 1.0, 0.0)
+        flags_out[8 * n : 8 * n + 8, :] = jnp.full((8, 128), even, F32)
     steps, rows, cols = obs_out.shape
     own_rows = rows - 2 * HALO
     own_cols = cols - 128
@@ -352,7 +357,7 @@
 
 
 def frame_kernel(
-    place_ref, eta_ref, depth_ref, wet_ref, fric_ref, one_in, two_in, dde, rre, wwe, fe, fs, *refs
+    flags_ref, eta_ref, depth_ref, wet_ref, fric_ref, one_in, two_in, dde, rre, wwe, fe, fs, *refs
 ):
     east, south = refs[:6], refs[6:12]
     surf0, wet, surf1, fe1, ae1, pe1, qe1 = refs[12:19]
@@ -360,10 +365,10 @@
     rows, cols = eta_ref.shape
     fields = (depth_ref, wet_ref, fric_ref, eta_ref)
     blocks = rows // 8
-    gy = place_ref[1]
+    flags = flags_ref[...]
     for n, side in enumerate(sides):
         one, two = one_in[8 * n : 8 * n + 8], two_in[8 * n : 8 * n + 8]
-        side[...] = side_block(by_parity(gy, one, two), by_parity(gy, two, one))
+        side[...] = side_block(choose(flags, 1, one, two), choose(flags, 1, two, one))
 
     def frame(i, c):
         at = rows_at(i)
@@ -416,13 +421,13 @@
 
 
 def solve_kernel(*refs):
-    place_ref, grow_ref, gcol_ref = refs[:3]
+    late = refs[:3] + (refs[42],)
     east0, south0, east_part, south_part = (refs[3 + 6 * n : 9 + 6 * n] for n in range(4))
     surf0, wet, surf1, fe1, ae1, pe1, qe1 = refs[27:34]
-    one_in, two_in, top_ref, bottom_ref, count, obs, recv, block_ref = refs[34:42]
-    final_ref, adj_ref, back_ref = refs[42:45]
+    flags_ref, one_in, two_in, top_ref, bottom_ref, count, obs, recv, _ = refs[34:43]
+    final_ref, adj_ref, back_ref = refs[43:46]
     steps, rows, cols = obs.shape
-    scratch = list(refs[45:])
+    scratch = list(refs[46:])
 
     def take_scratch(n):
         taken = scratch[:n]
@@ -439,9 +444,17 @@
     qe = [qe0, qe1] + take_scratch(steps - 2)
     ps = [ps0] + take_scratch(steps - 1)
     qs = [qs0] + take_scratch(steps - 1)
-    adj, ce, cs, spread, turned, west, xe, xs, grads, parts, reads, north_ref, south_ref = scratch
-    south_ref[...] = by_parity(place_ref[0], one_in[...], two_in[...])
-    north_ref[...] = by_parity(place_ref[0], two_in[...], one_in[...])
+    adj, ce, cs, spread, turned, west, xe, xs, grads, parts, reads, north_ref, south_ref = scratch[:-5]
+    place_ref, grow_ref, gcol_ref, block_ref, sems = scratch[-5:]
+    loads = [
+        pltpu.make_async_copy(src, dst, sems.at[n])
+        for n, (src, dst) in enumerate(zip(late, scratch[-5:-1]))
+    ]
+    for load in loads:
+        load.start()
+    flags = flags_ref[...]
+    south_ref[...] = choose(flags, 0, one_in[...], two_in[...])
+    north_ref[...] = choose(flags, 0, two_in[...], one_in[...])
     sub = row_iota((8, cols))
     last = sub == 7
     firstrow = sub == 0
@@ -573,6 +586,8 @@
 
     final_ref[...] = surf[steps][HALO : HALO + own_rows, 0:own_cols]
 
+    for load in loads:
+        load.wait()
     gx, gy = place_ref[0], place_ref[1]
     lane8 = lax.broadcasted_iota(I32, (8, 128), 1)
     sub8 = row_iota((8, 128))
@@ -755,9 +770,9 @@
     place = jnp.stack(
         [lax.axis_index("gx"), lax.axis_index("gy"), jnp.int32(width_x), jnp.int32(width_y)]
     ).astype(I32)
-    count, obs, token = pl.pallas_call(
+    count, obs, flags = pl.pallas_call(
         gauge_kernel,
-        out_shape=[grid, f((steps, rows, cols), F32), f((8, 128), F32)],
+        out_shape=[grid, f((steps, rows, cols), F32), f((16, 128), F32)],
         in_specs=[smem()] * 4,
         out_specs=[vmem()] * 3,
         name="gauges",
@@ -770,13 +785,13 @@
         + [f((32, rows_here), F32)] * 2
         + [f((32, cols_here), F32)] * 2
         + [f((8, devices), I32)],
-        in_specs=[smem()] + [vmem()] * 6 + [hbm()],
+        in_specs=[vmem()] * 7,
         out_specs=[vmem()] * 6,
         scratch_shapes=[pltpu.SMEM((8, devices), I32), pltpu.SemaphoreType.DMA]
         + [pltpu.VMEM((rows_here * cols_here // 1024, 8, 128), F32)] * SLOTS,
         name="scatter",
         compiler_params=pltpu.CompilerParams(vmem_limit_bytes=10 * MIB),
-    )(place, recv, wet_mask, *edges, token)
+    )(flags, recv, wet_mask, *edges)
     sides = swapped(one, "gy", 0), swapped(two, "gy", 1)
     tiles = (eta, ocean_depth, wet_mask, manning)
     made = pl.pallas_call(
@@ -790,28 +805,28 @@
     top, bottom, one, two = pl.pallas_call(
         rim_kernel,
         out_shape=[f((32, cols), F32)] * 4,
-        in_specs=[smem()] + [vmem()] * 4 + [hbm()],
+        in_specs=[vmem()] * 5 + [hbm()],
         out_specs=[vmem()] * 4,
         compiler_params=pltpu.CompilerParams(vmem_limit_bytes=MIB),
         name="rims",
-    )(place, *sides, top, bottom, made[0])
+    )(flags, *sides, top, bottom, made[0])
     ends = swapped(one, "gx", 0), swapped(two, "gx", 1)
     framed = pl.pallas_call(
         frame_kernel,
         out_shape=[f((rows, 256), F32)] * 6 + [f((rows, 128), F32)] * 6 + [grid] * 7,
-        in_specs=[smem()] + [vmem()] * 11,
+        in_specs=[vmem()] * 12,
         out_specs=[vmem()] * 19,
         scratch_shapes=[pltpu.VMEM((rows_here, 128), F32)] * 4,
         compiler_params=pltpu.CompilerParams(vmem_limit_bytes=2 * MIB),
         name="frame",
-    )(place, *tiles, *sides, *made[:4], made[9])
+    )(flags, *tiles, *sides, *made[:4], made[9])
 
     tile = f((rows_here, cols_here), F32)
 
     final, adjoint, back = pl.pallas_call(
         solve_kernel,
         out_shape=[tile, tile, f((devices, 128), F32)],
-        in_specs=[smem()] * 3 + [vmem()] * 38 + [smem()],
+        in_specs=[hbm()] * 3 + [vmem()] * 39 + [hbm()],
         out_specs=[vmem()] * 3,
         scratch_shapes=[pltpu.VMEM((rows, cols), F32)] * (4 * (steps - 1) + 3 * (steps - 2) + 8)
         + [
@@ -819,12 +834,14 @@
             pltpu.VMEM((SLOTS, devices, 128), F32),
             pltpu.VMEM((steps * per_tile, 128), F32),
         ]
-        + [pltpu.VMEM((32, cols), F32)] * 2,
+        + [pltpu.VMEM((32, cols), F32)] * 2
+        + [pltpu.SMEM(v.shape, I32) for v in (place, gauge_row, gauge_col, block_of)]
+        + [pltpu.SemaphoreType.DMA((4,))],
         compiler_params=pltpu.CompilerParams(vmem_limit_bytes=26 * MIB),
         name="solve",
     )(
         place, gauge_row, gauge_col, *made, *framed,
-        *ends, top, bottom, count, obs, recv, block_of,
+        flags, *ends, top, bottom, count, obs, recv, block_of,
     )
     returned = lax.all_to_all(back, both, split_axis=0, concat_axis=0, tiled=True)
     readings, grad_slip = pl.pallas_call(

time: 101 us -> 99.3 us (0.983)
  Pallas kernels: 38.4 us -> 36.1 us
where the time goes in v5:
time: 99.3 us; the launch traced here: 99 us
  Pallas kernels  36.1 us (36%)
  waiting for transfers between devices  23.2 us (23%)
  blocking collectives  17.7 us (18%)
  starting transfers between devices  17.5 us (18%)
  local copies, waits for them, and re-layouts  3.55 us (4%)
    all_to_all x1, waiting for transfers between devices, body(): lax.all_to_all(packed.reshape(-1), both, split_axis=0, concat_axis=0, til...  21.3 us
    pallas_call x1, Pallas kernels, body(): pl.pallas_call(solve_kernel, out_shape=[tile, tile, f((devices, 128), F32...  18.7 us
    all_to_all x1, blocking collectives, body(): lax.all_to_all(back, both, split_axis=0, concat_axis=0, tiled=True)  17.7 us
    all_to_all x1, starting transfers between devices, body(): lax.all_to_all(packed.reshape(-1), both, split_axis=0, concat_axis=0, til...  11.5 us
    ppermute x4, starting transfers between devices, swapped(): return lax.ppermute(shard, axis, pairs + [(j, i) for i, j in pairs])  6 us
    pallas_call x1, Pallas kernels, body(): pl.pallas_call(gauge_kernel, out_shape=[grid, f((steps, rows, cols), F32)...  5.14 us
    pallas_call x1, Pallas kernels, body(): pl.pallas_call(pack_kernel, out_shape=[f((devices * CHUNK, 128), F32), f(...  3.59 us
    unnamed x26, local copies, waits for them, and re-layouts  3.55 us
  transfers between devices with their start and end apart: 5, of which 2 were waited for; matrix products, arithmetic and copies ran while one was open for 0% of the time, Pallas kernels for 11%

profile of v5, /device:TPU:1, one launch (start us, length us, event | category | flops | bytes accessed | tf_op | source)
XLA Modules:
  0.0 99.0 jit_solution(17407151741350274407)
XLA Ops:
  0.6 3.6 %pack.1 = (f32[4224,128]{1,0:T(8,128)}, f32[128,128]{1,0:T(8,128)}) custom-call(f32[16]{0:T(128)} %slip_ref.3, s32[1,256]{1,0:T(1,128)} %bitcast.15, s32[1,256]{1,0:T(1,128)} %bitcast.16, f32[256,8,128]{2,1,0:T(8,128)} %pattern_hbm.1), custom_call_target="tpu_custom_call" | custom-call | tf_op jit(solution)/shard_map/pack/pallas_call | solution.py:744
  4.2 0.0 copy-start
  4.2 0.0 copy-start.1
  4.3 0.0 copy-start.9
  4.3 0.0 copy-start.10
  4.3 0.0 copy-start.11
  4.3 11.5 %all-to-all-start = ((f32[128,4224,1]{1,2,0:T(1,128)}), f32[128,4224,1]{1,2,0:T(1,128)S(1)}, u32[]{:S(2)}, u32[]{:S(2)}) async-start(f32[128,4224,1]{1,2,0:T(1,128)} %bitcast.14), calls=%async_computation | async-start | bytes 4325376 | tf_op jit(solution)/shard_map/all_to_all | solution.py:757
  15.8 0.0 copy-start.2
  15.8 1.0 %copy-done.2 = f32[256,512]{1,0:T(8,128)S(1)} copy-done((f32[256,512]{1,0:T(8,128)S(1)}, f32[256,512]{1,0:T(8,128)}, u32[]{:S(2)}) %copy-start.2) | copy-done | bytes 524312
  16.9 0.1 static_edges.1
  17.0 0.1 pad_add_fusion.place_ref.refs_0_
  17.1 0.0 copy-done.9
  17.1 0.0 copy-done.11
  17.1 5.1 %gauges.1 = (f32[272,640]{1,0:T(8,128)S(1)}, f32[4,272,640]{2,1,0:T(8,128)S(1)}, f32[16,128]{1,0:T(8,128)S(1)}) custom-call(s32[4]{0:T(128)S(1)} %pad_add_fusion.place_ref.refs_0_, s32[2048]{0:T(1024)S(1)} %copy-done.9, s32[2048]{0:T(1024)S(1)} %copy-done.10, f32[4,2048]{1,0:T(4,128)S(1)} %copy-done.11), custom_call_target="tpu_custom_call" | custom-call | tf_op jit(solution)/shard_map/gauges/pallas_call | solution.py:773
  22.3 1.6 %copy-done.4 = f32[4,272,640]{2,1,0:T(8,128)} copy-done((f32[4,272,640]{2,1,0:T(8,128)}, f32[4,272,640]{2,1,0:T(8,128)S(1)}, u32[]{:S(2)}) %copy-start.4) | copy-done | bytes 2785304
  23.8 0.9 copy-done.6
  24.7 21.3 %all-to-all-done = f32[128,4224,1]{1,2,0:T(1,128)S(1)} async-done(((f32[128,4224,1]{1,2,0:T(1,128)}), f32[128,4224,1]{1,2,0:T(1,128)S(1)}, u32[]{:S(2)}, u32[]{:S(2)}) %all-to-all-start) | async-done | bytes 2162720 | tf_op jit(solution)/shard_map/all_to_all | solution.py:757
  46.0 1.9 %scatter.1 = (f32[256,512]{1,0:T(8,128)S(1)}, f32[32,256]{1,0:T(8,128)S(1)}, f32[32,256]{1,0:T(8,128)S(1)}, f32[32,512]{1,0:T(8,128)S(1)}, f32[32,512]{1,0:T(8,128)S(1)}, /*index=5*/s32[8,128]{1,0:T(8,128)S(1)}) custom-call(f32[16,128]{1,0:T(8,128)S(1)} %get-tuple-element.59.flags_ref.refs_34_, f32[4224,128]{1,0:T(8,128)S(1)} %bitcast.10, ...), custom_call_target="tpu_custom_call" | custom-call | tf_op jit(solution)/shard_map/scatter/pallas_call | solution.py:782
  48.0 0.5 collective-permute-start
  48.5 0.7 collective-permute-start.1
  49.2 2.3 %tile.1 = (f32[272,640]{1,0:T(8,128)S(1)}, f32[272,640]{1,0:T(8,128)S(1)}, f32[272,640]{1,0:T(8,128)S(1)}, f32[272,640]{1,0:T(8,128)S(1)}, f32[272,640]{1,0:T(8,...) custom-call(f32[256,512]{1,0:T(8,128)S(1)} %get-tuple-element.65.eta, ...), custom_call_target="tpu_custom_call" | custom-call | tf_op jit(solution)/shard_map/tile/pallas_call | solution.py:797
  51.5 0.0 collective-permute-done.one_in
  51.5 0.0 collective-permute-done.1.two_in
  51.5 0.2 rims.1
  51.7 2.4 %collective-permute-start.2 = (f32[32,640]{1,0:T(8,128)S(1)}, f32[32,640]{1,0:T(8,128)S(1)}, u32[]{:S(2)}, u32[]{:S(2)}) collective-permute-start(f32[32,640]{1,0:T(8,128)S(1)} %get-tuple-element.101), channel_id=1, source_target_pairs={{0,8},{16,24},{32,40},{48,56},{64,72},{80,88},{96,104},{112,120},{... | collective-permute-start | bytes 245768 | tf_op jit(solution)/shard_map/ppermute | solution.py:43
  54.1 2.4 %collective-permute-start.3 = (f32[32,640]{1,0:T(8,128)S(1)}, f32[32,640]{1,0:T(8,128)S(1)}, u32[]{:S(2)}, u32[]{:S(2)}) collective-permute-start(f32[32,640]{1,0:T(8,128)S(1)} %get-tuple-element.102), channel_id=1, source_target_pairs={{8,16},{24,32},{40,48},{56,64},{72,80},{88,96},{104,112},{16,8},{3... | collective-permute-start | bytes 245768 | tf_op jit(solution)/shard_map/ppermute | solution.py:43
  56.5 3.2 %frame.1 = (f32[272,256]{1,0:T(8,128)S(1)}, f32[272,256]{1,0:T(8,128)S(1)}, f32[272,256]{1,0:T(8,128)S(1)}, f32[272,256]{1,0:T(8,128)S(1)}, f32[272,256]{1,0:T(8...) custom-call(f32[16,128]{1,0:T(8,128)S(1)} %get-tuple-element.59.flag, ...), custom_call_target="tpu_custom_call" | custom-call | tf_op jit(solution)/shard_map/frame/pallas_call | solution.py:814
  59.7 0.0 collective-permute-done.2.refs_35_
  59.7 1.9 %collective-permute-done.3.refs_36_ = f32[32,640]{1,0:T(8,128)S(1)} collective-permute-done((f32[32,640]{1,0:T(8,128)S(1)}, f32[32,640]{1,0:T(8,128)S(1)}, u32[]{:S(2)}, u32[]{:S(2)}) %collective-permute-start.3) | collective-permute-done | bytes 81952 | tf_op jit(solution)/shard_map/ppermute | solution.py:43
  61.6 18.7 %solve.1 = (f32[256,512]{1,0:T(8,128)}, f32[256,512]{1,0:T(8,128)}, f32[128,128]{1,0:T(8,128)S(1)}) custom-call(s32[4]{0:T(128)S(1)} %pad_add_fusion.place_ref.refs_0_, s32[2048]{0:T(1024)S(1)} %copy-done.9, s32[2048]{0:T(1024)S(1)} %copy-done.10, f32[272,640]{1,0:T(8,128)S(1)} %get-tuple-element.66.dde.after.refs_3_, ...), custom_call_target="tpu_custom_call" | custom-call | tf_op jit(solution)/shard_map/solve/pallas_call | solution.py:826
  80.3 17.7 %all_to_all.20 = f32[128,1,128]{2,1,0:T(1,128)S(1)} all-to-all(f32[128,1,128]{2,1,0:T(1,128)S(1)} %bitcast.13), channel_id=1, replica_groups=mesh['gx'=16,'gy'=8] {'gx','gy'}, dimensions={0} | all-to-all | bytes 131072 | tf_op jit(solution)/shard_map/all_to_all | solution.py:846
  98.1 0.9 closing.1
  (15 shorter events, 0.0 us)
Async XLA Ops:
  4.2 11.6 %copy-start = (s32[256,512]{1,0:T(8,128)S(1)}, s32[256,512]{1,0:T(8,128)}, u32[]{:S(2)}) copy-start(s32[256,512]{1,0:T(8,128)} %wet_ref.7) | copy-start | bytes 1572868
  4.2 11.6 %copy-start.1 = (f32[256,512]{1,0:T(8,128)S(1)}, f32[256,512]{1,0:T(8,128)}, u32[]{:S(2)}) copy-start(f32[256,512]{1,0:T(8,128)} %depth_ref.5) | copy-start | bytes 1572868
  4.3 12.8 %copy-start.9 = (s32[2048]{0:T(1024)S(1)}, s32[2048]{0:T(1024)}, u32[]{:S(2)}) copy-start(s32[2048]{0:T(1024)} %refs_1_.1) | copy-start | bytes 24580
  4.3 12.8 %copy-start.10 = (s32[2048]{0:T(1024)S(1)}, s32[2048]{0:T(1024)}, u32[]{:S(2)}) copy-start(s32[2048]{0:T(1024)} %refs_2_.1) | copy-start | bytes 24580
  4.3 12.8 %copy-start.11 = (f32[4,2048]{1,0:T(4,128)S(1)}, f32[4,2048]{1,0:T(4,128)}, u32[]{:S(2)}) copy-start(f32[4,2048]{1,0:T(4,128)} %obs_ref.1) | copy-start | bytes 98308
  4.3 41.7 %all-to-all-start = ((f32[128,4224,1]{1,2,0:T(1,128)}), f32[128,4224,1]{1,2,0:T(1,128)S(1)}, u32[]{:S(2)}, u32[]{:S(2)}) async-start(f32[128,4224,1]{1,2,0:T(1,128)} %bitcast.14), calls=%async_computation | async-start | bytes 4325376 | tf_op jit(solution)/shard_map/all_to_all | solution.py:757
  15.8 1.0 %copy-start.2 = (f32[256,512]{1,0:T(8,128)S(1)}, f32[256,512]{1,0:T(8,128)}, u32[]{:S(2)}) copy-start(f32[256,512]{1,0:T(8,128)} %fric_ref.5) | copy-start | bytes 1572868
  22.3 1.6 %copy-start.4 = (f32[4,272,640]{2,1,0:T(8,128)}, f32[4,272,640]{2,1,0:T(8,128)S(1)}, u32[]{:S(2)}) copy-start(f32[4,272,640]{2,1,0:T(8,128)S(1)} %get-tuple-element.106.refs_40_) | copy-start | bytes 8355844
  23.8 0.9 copy-start.6
  46.0 3.2 %copy-start.3 = (f32[256,512]{1,0:T(8,128)S(1)}, f32[256,512]{1,0:T(8,128)}, u32[]{:S(2)}) copy-start(f32[256,512]{1,0:T(8,128)} %fric_ref.5) | copy-start | bytes 1572868
  48.0 3.5 %collective-permute-start = (f32[32,256]{1,0:T(8,128)S(1)}, f32[32,256]{1,0:T(8,128)S(1)}, u32[]{:S(2)}, u32[]{:S(2)}) collective-permute-start(f32[32,256]{1,0:T(8,128)S(1)} %get-tuple-element.78), channel_id=1, source_target_pairs={{0,1},{2,3},{4,5},{6,7},{1,0},{3,2},{5,4},{7,6},{8,9},{10,11},{12,... | collective-permute-start | bytes 98312 | tf_op jit(solution)/shard_map/ppermute | solution.py:43
  48.5 3.0 %collective-permute-start.1 = (f32[32,256]{1,0:T(8,128)S(1)}, f32[32,256]{1,0:T(8,128)S(1)}, u32[]{:S(2)}, u32[]{:S(2)}) collective-permute-start(f32[32,256]{1,0:T(8,128)S(1)} %get-tuple-element.79), channel_id=1, source_target_pairs={{1,2},{3,4},{5,6},{2,1},{4,3},{6,5},{9,10},{11,12},{13,14},{10,9},... | collective-permute-start | bytes 98312 | tf_op jit(solution)/shard_map/ppermute | solution.py:43
  51.7 8.0 %collective-permute-start.2 = (f32[32,640]{1,0:T(8,128)S(1)}, f32[32,640]{1,0:T(8,128)S(1)}, u32[]{:S(2)}, u32[]{:S(2)}) collective-permute-start(f32[32,640]{1,0:T(8,128)S(1)} %get-tuple-element.101), channel_id=1, source_target_pairs={{0,8},{16,24},{32,40},{48,56},{64,72},{80,88},{96,104},{112,120},{... | collective-permute-start | bytes 245768 | tf_op jit(solution)/shard_map/ppermute | solution.py:43
  54.1 7.5 %collective-permute-start.3 = (f32[32,640]{1,0:T(8,128)S(1)}, f32[32,640]{1,0:T(8,128)S(1)}, u32[]{:S(2)}, u32[]{:S(2)}) collective-permute-start(f32[32,640]{1,0:T(8,128)S(1)} %get-tuple-element.102), channel_id=1, source_target_pairs={{8,16},{24,32},{40,48},{56,64},{72,80},{88,96},{104,112},{16,8},{3... | collective-permute-start | bytes 245768 | tf_op jit(solution)/shard_map/ppermute | solution.py:43
  56.5 5.1 %copy-start.5 = (f32[4,272,640]{2,1,0:T(8,128)S(1)}, f32[4,272,640]{2,1,0:T(8,128)}, u32[]{:S(2)}) copy-start(f32[4,272,640]{2,1,0:T(8,128)} %copy-done.4) | copy-start | bytes 8355844
  56.5 5.1 %copy-start.7 = (f32[272,640]{1,0:T(8,128)S(1)}, f32[272,640]{1,0:T(8,128)}, u32[]{:S(2)}) copy-start(f32[272,640]{1,0:T(8,128)} %copy-done.6) | copy-start | bytes 2088964
  61.6 36.4 %copy-start.8 = (f32[128,128]{1,0:T(8,128)S(1)}, f32[128,128]{1,0:T(8,128)}, u32[]{:S(2)}) copy-start(f32[128,128]{1,0:T(8,128)} %get-tuple-element.110.table_ref) | copy-start | bytes 196612
  61.6 36.4 %copy-start.12 = (f32[16]{0:T(128)S(1)}, f32[16]{0:T(128)}, u32[]{:S(2)}) copy-start(f32[16]{0:T(128)} %slip_ref.3) | copy-start | bytes 196
